TPU v7x, 512 devices: a whole 4x8x8 slice. The times are simulated.
512 devices in a mesh: req: 128 (over y, z, core), fsdp: 4 (over x).
Axes of the slice: x: 4, y: 8, z: 8, core: 2. Of those that a mesh axis runs over, the one named last changes fastest.
Arguments:
- tokens: bfloat16 [1024, 2048], P(('req', 'fsdp')), may hold values from -120 to 120, as said below
- cache_lengths: int32 [1024], P(('req', 'fsdp')), may hold values from 1 to 768, as said below
- kv_cache: bfloat16 [1, 1024, 768, 640], P(None, ('req', 'fsdp')), may hold values from -400 to 400, as said below
- attn_gain: float32 [1, 2048], replicated, may hold values from 0.1 to 1.9
- mlp_gain: float32 [1, 2048], replicated, may hold values from 0.1 to 1.9
- w_qkv: bfloat16 [1, 2048, 1920], P(None, 'req', 'fsdp'), may hold values from -0.125 to 0.125
- w_out: bfloat16 [1, 1280, 2048], P(None, 'req', 'fsdp'), may hold values from -0.15625 to 0.15625
- w_gate: bfloat16 [1, 2048, 2560], P(None, None, ('req', 'fsdp')), may hold values from -0.125 to 0.125
- w_up: bfloat16 [1, 2048, 2560], P(None, None, ('req', 'fsdp')), may hold values from -0.125 to 0.125
- w_down: bfloat16 [1, 2560, 2048], P(None, ('req', 'fsdp')), may hold values from -0.125 to 0.125
Outputs:
- stream_out: bfloat16 [1024, 2048], P(('req', 'fsdp'))
- new_kv: bfloat16 [1, 1024, 640], P(None, ('req', 'fsdp'))
Inputs may be any that keep to these rules, and one draw needn't show every extreme that they name: `cache_lengths`: a request's count of cached tokens; in every draw some request has exactly 768. `tokens`: real-valued activations. `kv_cache`: real-valued cached keys and values.
All inputs are finite; a program needn't handle non-finite values.
Results may differ from a plain program's by a relative error of at most 0.0052.
Values may be sent and summed in bfloat16 or wider, within the bound.
A program may use at most 64 MiB of HBM per device.

v0:
```python
import math

import jax
import jax.numpy as jnp
from jax import lax
from jax.sharding import PartitionSpec as P

H = 20
KVH = 5
HD = 64
CAP = 768
W = 384
SINKS = 4


def normed(values, gain):
    wide = values.astype(jnp.float32)
    return wide * lax.rsqrt(jnp.mean(wide * wide, axis=-1, keepdims=True) + 1e-05) * gain


def rotate(tensor, positions):
    half_width = tensor.shape[-1] // 2
    freqs = jnp.exp(
        jnp.arange(half_width, dtype=jnp.float32) * (-2.0 * math.log(10000.0) / tensor.shape[-1])
    )
    angles = positions.astype(jnp.float32)[:, None] * freqs[None, :]
    cosine = jnp.cos(angles)[:, None, :]
    sine = jnp.sin(angles)[:, None, :]
    first = tensor[..., :half_width]
    second = tensor[..., half_width:]
    return jnp.concatenate(
        [first * cosine - second * sine, second * cosine + first * sine], axis=-1
    )


def attend(queries, keys_all, values_all, visible, key_new, value_new):
    batch = queries.shape[0]
    grouped = queries.reshape(batch, KVH, H // KVH, HD)
    factor = HD ** (-0.5)
    scores = (
        jnp.einsum("rkgd,rckd->rkgc", grouped, keys_all, preferred_element_type=jnp.float32)
        * factor
    )
    own_score = (
        jnp.einsum("rkgd,rkd->rkg", grouped, key_new, preferred_element_type=jnp.float32) * factor
    )
    scores = jnp.where(visible[:, None, None, :], scores, -jnp.inf)
    peak = jnp.maximum(jnp.max(scores, axis=-1), own_score)
    weights = jnp.exp(scores - peak[..., None])
    own_weight = jnp.exp(own_score - peak)
    denom = jnp.sum(weights, axis=-1) + own_weight
    probs = (weights / denom[..., None]).astype(jnp.bfloat16)
    own_prob = (own_weight / denom).astype(jnp.bfloat16)
    mixed = jnp.einsum("rkgc,rckd->rkgd", probs, values_all, preferred_element_type=jnp.float32)
    mixed = (
        mixed
        + own_prob.astype(jnp.float32)[..., None] * value_new.astype(jnp.float32)[:, :, None, :]
    )
    return mixed.reshape(batch, H * HD).astype(jnp.bfloat16)


def swiglu(rows_in, gate_weight, up_weight):
    gate = jnp.dot(rows_in, gate_weight, preferred_element_type=jnp.float32)
    upward = jnp.dot(rows_in, up_weight, preferred_element_type=jnp.float32)
    return (jax.nn.silu(gate) * upward).astype(jnp.bfloat16)


def body(tokens, cache_lengths, kv_cache, attn_gain, mlp_gain, w_qkv, w_out, w_gate, w_up, w_down):
    own_rows = tokens.shape[0]
    n_query = H * HD
    n_key = KVH * HD
    stream = tokens
    lengths_col = cache_lengths[:, None]
    qkv_weight = lax.all_gather(w_qkv[0], "req", axis=0, tiled=True)
    out_weight = lax.all_gather(w_out[0], "req", axis=0, tiled=True)
    normed_rows = normed(stream, attn_gain[0]).astype(jnp.bfloat16)
    joint_part = jnp.dot(
        lax.all_gather(normed_rows, "fsdp", axis=0, tiled=True),
        qkv_weight,
        preferred_element_type=jnp.float32,
    )
    joint = lax.all_to_all(joint_part, "fsdp", split_axis=0, concat_axis=1, tiled=True)
    queries = rotate(joint[:, :n_query].reshape(own_rows, H, HD), cache_lengths).astype(
        jnp.bfloat16
    )
    key_new = rotate(
        joint[:, n_query : n_query + n_key].reshape(own_rows, KVH, HD), cache_lengths
    ).astype(jnp.bfloat16)
    value_new = joint[:, n_query + n_key :].reshape(own_rows, KVH, HD).astype(jnp.bfloat16)
    fresh_list = [
        jnp.concatenate(
            [key_new.reshape(own_rows, n_key), value_new.reshape(own_rows, n_key)], axis=1
        )
    ]
    layer_cache = kv_cache[0]
    positions = jnp.broadcast_to(jnp.arange(CAP, dtype=jnp.int32)[None, :], (own_rows, CAP))
    distinct = jnp.ones((own_rows, CAP), dtype=bool)
    visible = (
        distinct & (positions < lengths_col) & ((positions < SINKS) | (positions > lengths_col - W))
    )
    slot_count = layer_cache.shape[1]
    keys_all = layer_cache[..., :n_key].reshape(own_rows, slot_count, KVH, HD)
    values_all = layer_cache[..., n_key:].reshape(own_rows, slot_count, KVH, HD)
    context = attend(queries, keys_all, values_all, visible, key_new, value_new)
    projected_part = jnp.dot(
        lax.all_gather(context, "fsdp", axis=0, tiled=True),
        out_weight,
        preferred_element_type=jnp.float32,
    )
    projected = lax.all_to_all(projected_part, "fsdp", split_axis=0, concat_axis=1, tiled=True)
    after_attn = (stream.astype(jnp.float32) + projected).astype(jnp.bfloat16)
    second = normed(after_attn, mlp_gain[0]).astype(jnp.bfloat16)
    gate_weight = lax.all_gather(w_gate[0], "req", axis=1, tiled=True)
    up_weight = lax.all_gather(w_up[0], "req", axis=1, tiled=True)
    down_weight = lax.all_gather(w_down[0], "req", axis=0, tiled=True)
    hidden = swiglu(lax.all_gather(second, "fsdp", axis=0, tiled=True), gate_weight, up_weight)
    down = lax.psum_scatter(
        jnp.dot(hidden, down_weight, preferred_element_type=jnp.float32),
        "fsdp",
        scatter_dimension=0,
        tiled=True,
    )
    stream = (after_attn.astype(jnp.float32) + down).astype(jnp.bfloat16)
    return (stream, jnp.stack(fresh_list))


def solution(mesh):
    return jax.shard_map(
        body,
        mesh=mesh,
        in_specs=(
            P(("req", "fsdp"), None),
            P(("req", "fsdp")),
            P(None, ("req", "fsdp"), None, None),
            P(),
            P(),
            P(None, "req", "fsdp"),
            P(None, "req", "fsdp"),
            P(None, None, ("req", "fsdp")),
            P(None, None, ("req", "fsdp")),
            P(None, ("req", "fsdp"), None),
        ),
        out_specs=(P(("req", "fsdp"), None), P(None, ("req", "fsdp"), None)),
        check_vma=False,
    )
```

profile of v0, /device:TPU:1, one launch (start us, length us, event | category | flops | bytes accessed | tf_op | source)
XLA Modules:
  0.0 498.7 jit_solution(18189808930634611015)
XLA Ops:
  7.2 0.7 all-gather.14.cloned.1.call-update
  7.9 1.3 copy.40
  9.4 1.4 copy.41
  10.8 1.4 copy.43
  12.3 1.4 copy.45
  13.7 0.8 fusion.30
  14.6 0.8 fusion.43
  15.4 10.2 %all-gather.5 = bf16[4,2,2048]{2,1,0:T(2,128)(2,1)S(1)} all-gather(bf16[1,2,2048]{2,1,0:T(2,128)(2,1)S(1)} %fusion.43), channel_id=1, replica_groups=mesh['req'=128,'fsdp'=4] {'fsdp'}, dimensions={0}, use_global_device_ids=true | all-gather | bytes 40960 | tf_op jit(solution)/shard_map/all_gather | solution.py:78
  25.6 0.7 fusion.51
  26.4 0.7 or_and_fusion
  27.1 2.2 fusion.50
  29.3 70.8 %all-gather.14.cloned.1.call-done = bf16[1,2048,480]{2,1,0:T(8,128)(2,1)} async-done(((bf16[1,16,480]{2,1,0:T(8,128)(2,1)}), bf16[1,2048,480]{2,1,0:T(8,128)(2,1)}) %all-gather.14.cloned.1.call-update) | async-done | bytes 1966096 | tf_op jit(solution)/shard_map/all_gather | solution.py:74
  100.1 2.0 fusion.7
  102.7 4.0 all-to-all-start
  108.0 1.3 dynamic-slice
  109.9 0.9 all-to-all-done
  112.9 9.1 %all-gather.6 = bf16[4,2,1280]{2,1,0:T(2,128)(2,1)S(1)} all-gather(bf16[1,2,1280]{2,1,0:T(2,128)(2,1)S(1)} %reshape.170), channel_id=1, replica_groups=mesh['req'=128,'fsdp'=4] {'fsdp'}, dimensions={0}, use_global_device_ids=true | all-gather | bytes 25600 | tf_op jit(solution)/shard_map/all_gather | solution.py:106
  122.1 61.5 %all-gather.16.cloned.1.call-done = bf16[1,1280,512]{2,0,1:T(2,128)(2,1)} async-done(((bf16[1,10,512]{2,0,1:T(2,128)(2,1)}), bf16[1,1280,512]{2,0,1:T(2,128)(2,1)}) %all-gather.16.cloned.1.call-update) | async-done | bytes 1310736 | tf_op jit(solution)/shard_map/all_gather | solution.py:75
  183.5 2.0 fusion.9
  186.2 3.9 all-to-all-start.1
  190.3 4.0 all-to-all-done.1
  194.6 9.1 %all-gather.7 = bf16[4,2,2048]{2,1,0:T(2,128)(2,1)S(1)} all-gather(bf16[1,2,2048]{2,1,0:T(2,128)(2,1)S(1)} %fusion.42), channel_id=1, replica_groups=mesh['req'=128,'fsdp'=4] {'fsdp'}, dimensions={0}, use_global_device_ids=true | all-gather | bytes 40960 | tf_op jit(solution)/shard_map/all_gather | solution.py:116
  203.7 65.2 %all-gather.18.cloned.1.call-done = bf16[1,2048,640]{1,0,2:T(2,128)(2,1)} async-done(((bf16[1,2048,5]{1,0,2:T(2,128)(2,1)}), bf16[1,2048,640]{1,0,2:T(2,128)(2,1)}) %all-gather.18.cloned.1.call-update) | async-done | bytes 2621456 | tf_op jit(solution)/shard_map/all_gather | solution.py:113
  268.9 11.1 %copy.42 = bf16[1,2048,640]{2,1,0:T(8,128)(2,1)} copy(bf16[1,2048,640]{1,0,2:T(2,128)(2,1)} %all-gather.18.cloned.1.call-done) | data formatting | bytes 5242880 | tf_op jit(solution)/shard_map/all_gather | solution.py:113
  280.0 74.0 %all-gather.20.cloned.1.call-done = bf16[1,2048,640]{1,0,2:T(2,128)(2,1)} async-done(((bf16[1,2048,5]{1,0,2:T(2,128)(2,1)}), bf16[1,2048,640]{1,0,2:T(2,128)(2,1)}) %all-gather.20.cloned.1.call-update) | async-done | bytes 2621456 | tf_op jit(solution)/shard_map/all_gather | solution.py:114
  354.0 9.6 %copy.44 = bf16[1,2048,640]{2,1,0:T(8,128)(2,1)S(1)} copy(bf16[1,2048,640]{1,0,2:T(2,128)(2,1)} %all-gather.20.cloned.1.call-done) | data formatting | bytes 5242880 | tf_op jit(solution)/shard_map/all_gather | solution.py:114
  363.6 2.2 fusion.5
  365.8 73.3 %all-gather.22.cloned.1.call-done = bf16[1,640,2048]{2,0,1:T(2,128)(2,1)} async-done(((bf16[1,5,2048]{2,0,1:T(2,128)(2,1)}), bf16[1,640,2048]{2,0,1:T(2,128)(2,1)}) %all-gather.22.cloned.1.call-update) | async-done | bytes 2621456 | tf_op jit(solution)/shard_map/all_gather | solution.py:115
  439.0 4.9 fusion
  444.0 0.7 maximum_bitcast_fusion
  444.6 45.8 %all-reduce.3.cloned.1.call-done = f32[8,2048]{1,0:T(8,128)} async-done(((f32[8,2048]{1,0:T(8,128)}), f32[8,2048]{1,0:T(8,128)}) %all-reduce.3.cloned.1.call-update) | async-done | bytes 65552
  490.4 1.5 fusion.37
  (53 shorter events, 5.3 us)
Async XLA Ops:
  7.2 92.9 %all-gather.14.cloned.1.call-start = ((), (), s32[]{:S(2)}) async-start(), calls=%async_computation.2 | async-start | bytes 2113536 | tf_op jit(solution)/shard_map/all_gather | solution.py:74
  7.9 175.6 %all-gather.16.cloned.1.call-start = ((), (), s32[]{:S(2)}) async-start(), calls=%async_computation.3 | async-start | bytes 2641920 | tf_op jit(solution)/shard_map/all_gather | solution.py:75
  9.3 259.6 %all-gather.18.cloned.1.call-start = ((), (), s32[]{:S(2)}) async-start(), calls=%async_computation.4 | async-start | bytes 5283840 | tf_op jit(solution)/shard_map/all_gather | solution.py:113
  10.8 343.2 %all-gather.20.cloned.1.call-start = ((), (), s32[]{:S(2)}) async-start(), calls=%async_computation.5 | async-start | bytes 5283840 | tf_op jit(solution)/shard_map/all_gather | solution.py:114
  12.3 426.8 %all-gather.22.cloned.1.call-start = ((), (), s32[]{:S(2)}) async-start(), calls=%async_computation.6 | async-start | bytes 5283840 | tf_op jit(solution)/shard_map/all_gather | solution.py:115
  102.7 8.2 %all-to-all-start = ((f32[4,2,480]{2,1,0:T(2,128)}), f32[4,2,480]{2,1,0:T(2,128)S(1)}, u32[]{:S(2)}, u32[]{:S(2)}) async-start(f32[4,2,480]{2,1,0:T(2,128)} %all_to_all.28), calls=%async_computation | async-start | bytes 32768 | tf_op jit(solution)/shard_map/all_to_all | solution.py:82
  108.0 86.4 %copy-start = (bf16[2,2048]{1,0:T(2,128)(2,1)S(1)}, bf16[2,2048]{1,0:T(2,128)(2,1)}, u32[]{:S(2)}) copy-start(bf16[2,2048]{1,0:T(2,128)(2,1)} %param.10) | copy-start | bytes 24580
  108.0 86.5 %copy-start.1 = (f32[1,2048]{1,0:T(1,128)S(1)}, f32[1,2048]{1,0:T(1,128)}, u32[]{:S(2)}) copy-start(f32[1,2048]{1,0:T(1,128)} %param.14) | copy-start | bytes 24580
  186.2 8.2 %all-to-all-start.1 = ((f32[4,2,512]{2,1,0:T(2,128)}), f32[4,2,512]{2,1,0:T(2,128)S(1)}, u32[]{:S(2)}, u32[]{:S(2)}) async-start(f32[4,2,512]{2,1,0:T(2,128)} %all_to_all.32), calls=%async_computation.1 | async-start | bytes 32768 | tf_op jit(solution)/shard_map/all_to_all | solution.py:110
  190.1 300.3 %all-reduce.3.cloned.1.call-start = ((), (), s32[]{:S(2)}) async-start(), calls=%async_computation.7 | async-start | bytes 131072
Sparse Core Ops, SparseCore 0:
  11.1 88.9 all-gather.13
  103.3 80.2 all-gather.15
  186.7 82.1 all-gather.17
  271.9 82.0 all-gather.19
  356.9 82.0 all-gather.21
  444.1 46.2 all-reduce.2
where the time goes:
time: 501 us; the launch traced here: 499 us
  waiting for transfers between devices  396 us (79%)
  local copies, waits for them, and re-layouts  32.9 us (7%)
  blocking collectives  28.4 us (6%)
  between operations  14.9 us (3%)
  matrix products  12.1 us (2%)
  starting transfers between devices  8.12 us (2%)
  other arithmetic  6.08 us (1%)
    all_gather x1, waiting for transfers between devices, body(): up_weight = lax.all_gather(w_up[0], 'req', axis=1, tiled=True)  74 us
    all_gather x1, waiting for transfers between devices, body(): down_weight = lax.all_gather(w_down[0], 'req', axis=0, tiled=True)  73.3 us
    all_gather x1, waiting for transfers between devices, body(): qkv_weight = lax.all_gather(w_qkv[0], 'req', axis=0, tiled=True)  70.8 us
    all_gather x1, waiting for transfers between devices, body(): gate_weight = lax.all_gather(w_gate[0], 'req', axis=1, tiled=True)  65.2 us
    all_gather x1, waiting for transfers between devices, body(): out_weight = lax.all_gather(w_out[0], 'req', axis=0, tiled=True)  61.5 us
    unnamed x7, waiting for transfers between devices  46.5 us
    all_gather x1, local copies, waits for them, and re-layouts, body(): gate_weight = lax.all_gather(w_gate[0], 'req', axis=1, tiled=True)  11.1 us
    all_gather x1, blocking collectives, body(): lax.all_gather(normed_rows, 'fsdp', axis=0, tiled=True)  10.2 us
  transfers between devices with their start and end apart: 8, of which 8 were waited for; matrix products, arithmetic and copies ran while one was open for 9% of the time, Pallas kernels for 0%

commit v1 on v0

v1 whole, which is shorter than its diff:
```python
import functools
import math

import jax
import jax.numpy as jnp
from jax import lax
from jax.experimental import pallas as pl
from jax.experimental.pallas import tpu as pltpu
from jax.sharding import PartitionSpec as P

H = 20
KVH = 5
HD = 64
CAP = 768
W = 384
SINKS = 4
DEVICES = 512
GROUP = 64
SHARDS = DEVICES // GROUP
TILE = 16
MESH = pl.DeviceIdType.MESH


def device(flat):
    return (lax.div(flat, 4), lax.rem(flat, 4))


def exchange_kernel(kinds, n_group, n_shard, *refs):
    n = n_group + n_shard
    srcs, dsts, (send, recv, own) = refs[:n], refs[n : 2 * n], refs[2 * n :]
    flat = lax.axis_index("req") * 4 + lax.axis_index("fsdp")
    member = lax.rem(flat, GROUP)
    base = flat - member
    shard = lax.div(flat, GROUP)

    def group_peer(i):
        return lax.rem(member + i, GROUP)

    def shard_peer(i):
        return lax.rem(shard + i, SHARDS) * GROUP + member

    barrier = pltpu.get_barrier_semaphore()

    def greet(i, c):
        pl.semaphore_signal(barrier, inc=1, device_id=device(base + group_peer(i)), device_id_type=MESH)
        return c

    def greet_shard(i, c):
        pl.semaphore_signal(barrier, inc=1, device_id=device(shard_peer(i)), device_id_type=MESH)
        return c

    lax.fori_loop(1, GROUP, greet, 0)
    count = GROUP - 1
    if n_shard:
        lax.fori_loop(1, SHARDS, greet_shard, 0)
        count += SHARDS - 1
    pl.semaphore_wait(barrier, count)

    def part(k, peer):
        if kinds[k] == "all":
            return srcs[k].at[peer]
        if kinds[k] == "quad":
            return srcs[k].at[lax.div(peer, 4)]
        return srcs[k].at[0]

    for k in range(n_group, n):

        def send_shard(i, c, k=k):
            pltpu.make_async_remote_copy(
                src_ref=srcs[k],
                dst_ref=dsts[k].at[shard],
                send_sem=send.at[k],
                recv_sem=recv.at[k],
                device_id=device(shard_peer(i)),
                device_id_type=MESH,
            ).start()
            return c

        lax.fori_loop(1, SHARDS, send_shard, 0)
        pltpu.make_async_copy(srcs[k], dsts[k].at[shard], own.at[k]).start()
    for k in range(n_group):

        def send_group(i, c, k=k):
            peer = group_peer(i)
            pltpu.make_async_remote_copy(
                src_ref=part(k, peer),
                dst_ref=dsts[k].at[member],
                send_sem=send.at[k],
                recv_sem=recv.at[k],
                device_id=device(base + peer),
                device_id_type=MESH,
            ).start()
            return c

        lax.fori_loop(1, GROUP, send_group, 0)
        pltpu.make_async_copy(part(k, member), dsts[k].at[member], own.at[k]).start()
    for k in range(n):
        slots = (GROUP if k < n_group else SHARDS) - 1
        others = dsts[k].at[pl.ds(0, slots)]
        if k < n_group:
            pltpu.make_async_copy(part(k, member), dsts[k].at[member], own.at[k]).wait()
        else:
            pltpu.make_async_copy(srcs[k], dsts[k].at[shard], own.at[k]).wait()
        pltpu.make_async_copy(others, others, send.at[k]).wait()
        pltpu.make_async_copy(others, others, recv.at[k]).wait()


def exchange(name, ident, group_items, shard_items=()):
    kinds = tuple(kind for kind, _ in group_items)
    arrays = [a for _, a in group_items] + list(shard_items)
    n_group, n_shard = len(group_items), len(shard_items)
    outs = [jax.ShapeDtypeStruct((GROUP,) + a.shape[1:], a.dtype) for _, a in group_items]
    outs += [jax.ShapeDtypeStruct((SHARDS,) + a.shape, a.dtype) for a in shard_items]
    n = n_group + n_shard
    return pl.pallas_call(
        functools.partial(exchange_kernel, kinds, n_group, n_shard),
        name=name,
        out_shape=outs,
        in_specs=[pl.BlockSpec(memory_space=pltpu.VMEM)] * n,
        out_specs=[pl.BlockSpec(memory_space=pltpu.VMEM)] * n,
        scratch_shapes=[pltpu.SemaphoreType.DMA((n,))] * 3,
        compiler_params=pltpu.CompilerParams(collective_id=ident, has_side_effects=True),
    )(*arrays)


def normed(values, gain):
    wide = values.astype(jnp.float32)
    return wide * lax.rsqrt(jnp.mean(wide * wide, axis=-1, keepdims=True) + 1e-05) * gain


def rotate(tensor, cosine, sine):
    half = tensor.shape[-1] // 2
    first = tensor[..., :half]
    second = tensor[..., half:]
    return jnp.concatenate(
        [first * cosine - second * sine, second * cosine + first * sine], axis=-1
    )


def attend(queries, cache, visible, key_new, value_new):
    batch = queries.shape[0]
    n_key = KVH * HD
    same = (jnp.arange(H)[:, None] // (H // KVH) == jnp.arange(KVH)[None, :])[None, :, :, None]
    spread = jnp.where(same, queries[:, :, None, :], 0).reshape(batch, H, n_key)
    factor = HD ** (-0.5)
    scores = (
        jnp.einsum("rhe,rce->rhc", spread, cache[..., :n_key], preferred_element_type=jnp.float32)
        * factor
    )
    own_score = (
        jnp.sum(spread.astype(jnp.float32) * key_new.reshape(batch, 1, n_key).astype(jnp.float32), axis=-1)
        * factor
    )
    scores = jnp.where(visible[:, None, :], scores, -jnp.inf)
    peak = jnp.maximum(jnp.max(scores, axis=-1), own_score)
    weights = jnp.exp(scores - peak[..., None])
    own_weight = jnp.exp(own_score - peak)
    denom = jnp.sum(weights, axis=-1) + own_weight
    probs = (weights / denom[..., None]).astype(jnp.bfloat16)
    own_prob = (own_weight / denom).astype(jnp.bfloat16)
    mixed = jnp.einsum("rhc,rce->rhe", probs, cache[..., n_key:], preferred_element_type=jnp.float32)
    mixed = mixed + own_prob.astype(jnp.float32)[..., None] * value_new.reshape(
        batch, 1, n_key
    ).astype(jnp.float32)
    mixed = jnp.sum(jnp.where(same, mixed.reshape(batch, H, KVH, HD), 0.0), axis=2)
    return mixed.reshape(batch, H * HD).astype(jnp.bfloat16)


def scatter_columns(rows, depth):
    quads = GROUP // 4
    cut = rows.reshape(2, SHARDS, quads, depth)
    cut = jnp.pad(cut, ((0, 0), (0, 0), (0, 0), (0, TILE - depth)))
    return cut.transpose(2, 0, 1, 3).reshape(quads, 2, SHARDS * TILE)


def summed(parts, width):
    total = jnp.sum(parts.reshape(GROUP // 4, 4, 2, parts.shape[-1]), axis=0)[..., :width]
    return total.transpose(1, 0, 2).reshape(2, 4 * width)


def body(tokens, cache_lengths, kv_cache, attn_gain, mlp_gain, w_qkv, w_out, w_gate, w_up, w_down):
    n_query = H * HD
    n_key = KVH * HD
    rows = GROUP * 2
    packed = SHARDS * TILE
    w_attn = jnp.concatenate(
        [jnp.pad(w_qkv[0], ((0, 0), (0, 32))), jnp.pad(w_out[0], ((0, 6), (0, 0)))], axis=1
    )
    w_ffn = jnp.concatenate(
        [w_gate[0].T, w_up[0].T, w_down[0], jnp.zeros((1, w_down.shape[2]), w_down.dtype)], axis=0
    )
    half_ffn = w_ffn.shape[1] // 2

    stream = tokens
    normed_rows = normed(stream, attn_gain[0]).astype(jnp.bfloat16)
    h_all, attn_all = exchange(
        "ex_h", 0, [("quad", scatter_columns(normed_rows, 16))], [w_attn]
    )
    attn_all = attn_all.reshape(packed, 1024)
    joint_part = jnp.dot(
        h_all.reshape(rows, packed), attn_all[:, :512], preferred_element_type=jnp.float32
    )
    joint_all, ffn_left = exchange(
        "ex_qkv", 1, [("all", joint_part.reshape(GROUP, 2, 512))], [w_ffn[:, :half_ffn]]
    )
    joint = summed(joint_all, 480)

    freqs = jnp.exp(
        jnp.arange(HD // 2, dtype=jnp.float32) * (-2.0 * math.log(10000.0) / HD)
    )
    angles = cache_lengths.astype(jnp.float32)[:, None] * freqs[None, :]
    cosine = jnp.cos(angles)[:, None, :]
    sine = jnp.sin(angles)[:, None, :]
    turned = rotate(
        joint[:, : n_query + n_key].reshape(2, H + KVH, HD), cosine, sine
    ).astype(jnp.bfloat16)
    queries, key_new = turned[:, :H], turned[:, H:]
    value_new = joint[:, n_query + n_key :].astype(jnp.bfloat16)
    fresh = jnp.concatenate([key_new.reshape(2, n_key), value_new], axis=1)
    lengths_col = cache_lengths[:, None]
    positions = jnp.arange(CAP, dtype=jnp.int32)[None, :]
    visible = (positions < lengths_col) & (
        (positions < SINKS) | (positions > lengths_col - W)
    )
    context = attend(queries, kv_cache[0], visible, key_new, value_new)

    ctx_all, ffn_right = exchange(
        "ex_ctx", 2, [("quad", scatter_columns(context, 10))], [w_ffn[:, half_ffn:]]
    )
    projected_part = jnp.dot(
        ctx_all.reshape(rows, packed), attn_all[:, 512:], preferred_element_type=jnp.float32
    )
    (projected_all,) = exchange("ex_out", 3, [("all", projected_part.reshape(GROUP, 2, 512))])
    projected = summed(projected_all, 512)
    after_attn = (stream.astype(jnp.float32) + projected).astype(jnp.bfloat16)
    second = normed(after_attn, mlp_gain[0]).astype(jnp.bfloat16)
    (second_all,) = exchange("ex_mlp", 4, [("one", second[None])])
    second_all = second_all.reshape(rows, 2 * half_ffn)
    ffn = jnp.concatenate(
        [ffn_left.reshape(packed, half_ffn), ffn_right.reshape(packed, half_ffn)], axis=1
    )
    gate_up = lax.dot_general(
        second_all, ffn, (((1,), (1,)), ((), ())), preferred_element_type=jnp.float32
    ).reshape(rows, SHARDS, TILE)
    hidden = (jax.nn.silu(gate_up[..., :5]) * gate_up[..., 5:10]).astype(jnp.bfloat16)
    hidden = jnp.pad(hidden, ((0, 0), (0, 0), (10, 1))).reshape(rows, packed)
    down_part = jnp.dot(hidden, ffn, preferred_element_type=jnp.float32).astype(jnp.bfloat16)
    (down_all,) = exchange("ex_down", 5, [("all", down_part.reshape(GROUP, 2, 2 * half_ffn))])
    down = jnp.sum(down_all.astype(jnp.float32), axis=0)
    stream = (after_attn.astype(jnp.float32) + down).astype(jnp.bfloat16)
    return (stream, fresh[None])


def solution(mesh):
    return jax.shard_map(
        body,
        mesh=mesh,
        in_specs=(
            P(("req", "fsdp"), None),
            P(("req", "fsdp")),
            P(None, ("req", "fsdp"), None, None),
            P(),
            P(),
            P(None, "req", "fsdp"),
            P(None, "req", "fsdp"),
            P(None, None, ("req", "fsdp")),
            P(None, None, ("req", "fsdp")),
            P(None, ("req", "fsdp"), None),
        ),
        out_specs=(P(("req", "fsdp"), None), P(None, ("req", "fsdp"), None)),
        check_vma=False,
    )
```

time: 501 us -> 152 us (0.30)
  waiting for transfers between devices: 396 us -> 0 us
  Pallas kernels: 0 us -> 122 us
  blocking collectives: 28.4 us -> 0 us
  local copies, waits for them, and re-layouts: 32.9 us -> 9.91 us
  between operations: 14.9 us -> 0.96 us
  starting transfers between devices: 8.12 us -> 0 us
  other arithmetic: 6.08 us -> 12.3 us
  matrix products: 12.1 us -> 5.9 us
    all_gather x5 -> x0, waiting for transfers between devices: 345 us -> none  [the longest x1 74 us: body(): up_weight = lax.all_gather(w_up[0], 'req', axis=1, tiled=True)]
    pallas_call x0 -> x6, Pallas kernels: none -> 122 us  [exchange(): pl.pallas_call(functools.partial(exchange_kernel, kinds, n_group, n_shard...]
    unnamed x7 -> x0, waiting for transfers between devices: 46.5 us -> none
    all_gather x3 -> x0, blocking collectives: 28.4 us -> none  [the longest x1 10.2 us: body(): lax.all_gather(normed_rows, 'fsdp', axis=0, tiled=True)]
    all_gather x2 -> x0, local copies, waits for them, and re-layouts: 20.7 us -> none  [the longest x1 11.1 us: body(): gate_weight = lax.all_gather(w_gate[0], 'req', axis=1, tiled=True)]
    all_to_all x2 -> x0, starting transfers between devices: 7.91 us -> none  [the longest x1 3.97 us: body(): lax.all_to_all(joint_part, 'fsdp', split_axis=0, concat_axis=1, tiled=True)]
    dot_general x7 -> x6, matrix products: 12.1 us -> 5.9 us  [the longest x1 1.65 us: attend(): jnp.einsum('rhc,rce->rhe', probs, cache[..., n_key:], preferred_element_t...]
  transfers between devices with their start and end apart: 8 -> 0, of which waited for: 8 -> 0; matrix products, arithmetic and copies ran while one was open for 9% -> 0% of each run, Pallas kernels for 0% -> 0%
where the time goes in v1:
time: 152 us; the launch traced here: 151 us
  Pallas kernels  122 us (80%)
  other arithmetic  12.3 us (8%)
  local copies, waits for them, and re-layouts  9.91 us (7%)
  matrix products  5.9 us (4%)
    pallas_call x6, Pallas kernels, exchange(): pl.pallas_call(functools.partial(exchange_kernel, kinds, n_group, n_shard...  122 us

profile of v1, /device:TPU:1, one launch (start us, length us, event | category | flops | bytes accessed | tf_op | source)
XLA Modules:
  0.0 150.7 jit_solution(9740125651521817174)
XLA Ops:
  0.6 1.0 fusion.22
  1.7 0.7 fusion.40
  2.6 0.7 or_and_fusion
  3.4 0.8 fusion.24
  4.4 1.3 fusion.18.refs_1_
  5.8 0.7 reshape.291.refs_0_
  6.5 0.9 maximum_maximum_fusion
  7.4 0.6 fusion.39
  8.0 25.4 %ex_h.1 = (bf16[64,2,128]{2,1,0:T(2,128)(2,1)}, bf16[8,16,1024]{2,1,0:T(8,128)(2,1)}) custom-call(bf16[16,2,128]{2,1,0:T(2,128)(2,1)} %reshape.291.refs_0_, bf16[16,1024]{1,0:T(8,128)(2,1)} %fusion.18.refs_1_), custom_call_target="tpu_custom_call" | custom-call | tf_op jit(solution)/shard_map/ex_h/pallas_call | solution.py:115
  33.5 1.1 fusion.11
  34.6 0.9 copy.59.refs_0_
  35.5 19.0 %ex_qkv.1 = (f32[64,2,512]{2,1,0:T(2,128)}, bf16[8,16,1024]{2,1,0:T(8,128)(2,1)}) custom-call(f32[64,2,512]{2,1,0:T(2,128)} %copy.59.refs_0_, bf16[16,1024]{1,0:T(8,128)(2,1)} %get-tuple-element.21.refs_1_), custom_call_target="tpu_custom_call" | custom-call | tf_op jit(solution)/shard_map/ex_qkv/pallas_call | solution.py:115
  54.5 1.0 reduce_sum.73
  56.2 0.7 maximum_bitcast_fusion
  57.4 2.4 %copy.62 = bf16[1,2,768,640]{2,3,1,0:T(8,128)(2,1)} copy(bf16[1,2,768,640]{3,2,1,0:T(8,128)(2,1)S(1)} %copy-done) | data formatting | bytes 3932160 | tf_op args[2]
  59.8 1.6 %fusion.41 = (f32[2,20]{1,0:T(2,128)S(1)}, f32[2,20,768]{2,1,0:T(8,128)S(1)}) fusion(bf16[2,768,640]{1,2,0:T(8,128)(2,1)} %bitcast.47, bf16[2,20,320]{2,0,1:T(2,128)(2,1)S(1)} %broadcast_select_fusion, pred[2,768]{1,0:T(4,128)(4,1)S(1)} %or_and_fusion), kind=kOutput, calls=%fused_computation.86 | convolution fusion | flops 19752920 | bytes 1133216 | tf_op jit(solution)/shard_map/rhe,rce->rhc/dot_general | solution.py:147
  61.6 1.6 %convolution_add_fusion = f32[2,20,320]{2,1,0:T(8,128)S(1)} fusion(bf16[2,768,640]{1,2,0:T(8,128)(2,1)} %bitcast.48, f32[2,20,768]{2,1,0:T(8,128)S(1)} %get-tuple-element.31, f32[2,20]{1,0:T(2,128)S(1)} %get-tuple-element.25, f32[2,20]{1,0:T(2,128)S(1)} %multiply_maximum_fusion, f32[2,320]{1,0:T(2,128)S(1)} %get-tuple-element.16, ...), kind=kOutput, calls=%fused_computation.3 | convolution fusion | flops 19778560 | bytes 1160160 | tf_op jit(solution)/shard_map/rhc,rce->rhe/dot_general | solution.py:161
  63.8 0.7 reshape.297.refs_0_
  64.5 12.9 %ex_ctx.1 = (bf16[64,2,128]{2,1,0:T(2,128)(2,1)}, bf16[8,16,1024]{2,1,0:T(8,128)(2,1)}) custom-call(bf16[16,2,128]{2,1,0:T(2,128)(2,1)} %reshape.297.refs_0_, bf16[16,1024]{1,0:T(8,128)(2,1)} %get-tuple-element.20.refs_1_), custom_call_target="tpu_custom_call" | custom-call | tf_op jit(solution)/shard_map/ex_ctx/pallas_call | solution.py:115
  77.5 1.0 fusion.10
  78.4 0.9 copy.69.refs_0_
  79.3 19.5 %ex_out.1 = f32[64,2,512]{2,1,0:T(2,128)} custom-call(f32[64,2,512]{2,1,0:T(2,128)} %copy.69.refs_0_), custom_call_target="tpu_custom_call" | custom-call | tf_op jit(solution)/shard_map/ex_out/pallas_call | solution.py:115
  98.9 1.0 reduce_sum.77
  100.1 0.7 fusion.31.refs_0_
  100.8 22.0 %ex_mlp.1 = bf16[64,2,2048]{2,1,0:T(2,128)(2,1)} custom-call(bf16[1,2,2048]{2,1,0:T(2,128)(2,1)} %fusion.31.refs_0_), custom_call_target="tpu_custom_call" | custom-call | tf_op jit(solution)/shard_map/ex_mlp/pallas_call | solution.py:115
  122.8 1.2 reshape.308
  124.0 0.3 fusion.3
  124.4 0.3 convolution_convert_fusion
  124.7 1.1 reshape.304.refs_0_
  125.9 22.8 %ex_down.1 = bf16[64,2,2048]{2,1,0:T(2,128)(2,1)} custom-call(bf16[64,2,2048]{2,1,0:T(2,128)(2,1)} %reshape.304.refs_0_), custom_call_target="tpu_custom_call" | custom-call | tf_op jit(solution)/shard_map/ex_down/pallas_call | solution.py:115
  148.6 1.5 convert_reduce_fusion
  150.1 0.6 fusion.29
  (53 shorter events, 2.6 us)
Async XLA Ops:
  0.6 56.7 %copy-start = (bf16[1,2,768,640]{3,2,1,0:T(8,128)(2,1)S(1)}, bf16[1,2,768,640]{3,2,1,0:T(8,128)(2,1)}, u32[]{:S(2)}) copy-start(bf16[1,2,768,640]{3,2,1,0:T(8,128)(2,1)} %param.12) | copy-start | bytes 5898244
  59.8 17.7 %copy-start.1 = (bf16[8,16,1024]{2,1,0:T(8,128)(2,1)S(1)}, bf16[8,16,1024]{2,1,0:T(8,128)(2,1)}, u32[]{:S(2)}) copy-start(bf16[8,16,1024]{2,1,0:T(8,128)(2,1)} %get-tuple-element.9) | copy-start | bytes 786436
  61.6 38.3 %copy-start.4 = (bf16[2,2048]{1,0:T(2,128)(2,1)S(1)}, bf16[2,2048]{1,0:T(2,128)(2,1)}, u32[]{:S(2)}) copy-start(bf16[2,2048]{1,0:T(2,128)(2,1)} %param.10) | copy-start | bytes 24580
  61.6 38.5 %copy-start.5 = (f32[1,2048]{1,0:T(1,128)S(1)}, f32[1,2048]{1,0:T(1,128)}, u32[]{:S(2)}) copy-start(f32[1,2048]{1,0:T(1,128)} %param.14) | copy-start | bytes 24580
  63.6 60.4 %copy-start.2 = (bf16[8,16,1024]{2,1,0:T(8,128)(2,1)S(1)}, bf16[8,16,1024]{2,1,0:T(8,128)(2,1)}, u32[]{:S(2)}) copy-start(bf16[8,16,1024]{2,1,0:T(8,128)(2,1)} %get-tuple-element.12) | copy-start | bytes 786436
  77.4 46.6 %copy-start.3 = (bf16[8,16,1024]{2,1,0:T(8,128)(2,1)S(1)}, bf16[8,16,1024]{2,1,0:T(8,128)(2,1)}, u32[]{:S(2)}) copy-start(bf16[8,16,1024]{2,1,0:T(8,128)(2,1)} %get-tuple-element.13) | copy-start | bytes 786436

commit v2 on v1

v2 whole, which is shorter than its diff:
```python
import math

import jax
import jax.numpy as jnp
from jax import lax
from jax.experimental import pallas as pl
from jax.experimental.pallas import tpu as pltpu
from jax.sharding import PartitionSpec as P

H = 20
KVH = 5
HD = 64
CAP = 768
W = 384
SINKS = 4
DEVICES = 512
GROUP = 64
SHARDS = DEVICES // GROUP
TILE = 16
MESH = pl.DeviceIdType.MESH


def device(flat):
    return (lax.div(flat, 4), lax.rem(flat, 4))


def place():
    flat = lax.axis_index("req") * 4 + lax.axis_index("fsdp")
    return lax.rem(flat, GROUP), lax.div(flat, GROUP)


def group_peer(member, shard, i):
    peer = lax.rem(member + i, GROUP)
    return peer, device(shard * GROUP + peer)


def shard_peer(member, shard, i):
    return device(lax.rem(shard + i, SHARDS) * GROUP + member)


def greet(member, shard):
    barrier = pltpu.get_barrier_semaphore()

    def in_group(i, c):
        pl.semaphore_signal(
            barrier, inc=1, device_id=group_peer(member, shard, i)[1], device_id_type=MESH
        )
        return c

    def in_shards(i, c):
        pl.semaphore_signal(
            barrier, inc=1, device_id=shard_peer(member, shard, i), device_id_type=MESH
        )
        return c

    lax.fori_loop(1, GROUP, in_group, 0)
    lax.fori_loop(1, SHARDS, in_shards, 0)
    pl.semaphore_wait(barrier, GROUP + SHARDS - 2)


class Transfer:
    def __init__(self, pick, dst, sems, k, member, shard, shards=False):
        self.pick, self.dst, self.member, self.shard, self.shards = pick, dst, member, shard, shards
        self.send, self.recv, self.own = (s.at[k] for s in sems)

    def local(self):
        mine = self.shard if self.shards else self.member
        return pltpu.make_async_copy(self.pick(self.member), self.dst.at[mine], self.own)

    def start(self):
        def step(i, c):
            if self.shards:
                peer, slot, target = i, self.shard, shard_peer(self.member, self.shard, i)
            else:
                peer, target = group_peer(self.member, self.shard, i)
                slot = self.member
            pltpu.make_async_remote_copy(
                src_ref=self.pick(peer),
                dst_ref=self.dst.at[slot],
                send_sem=self.send,
                recv_sem=self.recv,
                device_id=target,
                device_id_type=MESH,
            ).start()
            return c

        lax.fori_loop(1, SHARDS if self.shards else GROUP, step, 0)
        self.local().start()

    def arrive(self):
        others = self.dst.at[pl.ds(0, (SHARDS if self.shards else GROUP) - 1)]
        self.local().wait()
        pltpu.make_async_copy(others, others, self.recv).wait()

    def sent(self):
        others = self.dst.at[pl.ds(0, (SHARDS if self.shards else GROUP) - 1)]
        pltpu.make_async_copy(others, others, self.send).wait()


def head_kernel(h_ref, w_ref, joint_ref, w_all, h_all, part, part_all, *sems):
    member, shard = place()
    greet(member, shard)
    weights = Transfer(lambda peer: w_ref, w_all, sems, 0, member, shard, shards=True)
    rows = Transfer(lambda peer: h_ref.at[lax.div(peer, 4)], h_all, sems, 1, member, shard)
    parts = Transfer(lambda peer: part.at[peer], part_all, sems, 2, member, shard)
    weights.start()
    rows.start()
    rows.arrive()
    weights.arrive()
    product = jnp.dot(
        h_all[...].reshape(2 * GROUP, SHARDS * TILE),
        w_all[...].reshape(SHARDS * TILE, 1024)[:, :512],
        preferred_element_type=jnp.float32,
    )
    part[...] = product.astype(jnp.bfloat16).reshape(GROUP, 2, 512)
    parts.start()
    parts.arrive()
    joint_ref[...] = jnp.sum(
        part_all[...].astype(jnp.float32).reshape(GROUP // 4, 4, 2, 512), axis=0
    )
    weights.sent()
    rows.sent()
    parts.sent()


def tail_kernel(
    ctx_ref, w_out, w_ffn, tokens, gain, out_ref,
    ctx_all, part, part_all, second, second_all, down, down_all, ffn_all, *sems
):
    member, shard = place()
    greet(member, shard)
    rows = Transfer(lambda peer: ctx_ref.at[lax.div(peer, 4)], ctx_all, sems, 0, member, shard)
    weights = Transfer(lambda peer: w_ffn, ffn_all, sems, 1, member, shard, shards=True)
    parts = Transfer(lambda peer: part.at[peer], part_all, sems, 2, member, shard)
    seconds = Transfer(lambda peer: second, second_all, sems, 3, member, shard)
    downs = Transfer(lambda peer: down.at[peer], down_all, sems, 4, member, shard)
    packed = SHARDS * TILE
    rows.start()
    weights.start()
    rows.arrive()
    product = jnp.dot(
        ctx_all[...].reshape(2 * GROUP, packed),
        w_out[...].reshape(packed, 1024)[:, 512:],
        preferred_element_type=jnp.float32,
    )
    part[...] = product.astype(jnp.bfloat16).reshape(GROUP, 2, 512)
    parts.start()
    parts.arrive()
    projected = jnp.sum(
        part_all[...].astype(jnp.float32).reshape(GROUP // 4, 4, 2, 512), axis=0
    )
    projected = jnp.concatenate([projected[x] for x in range(4)], axis=-1)
    after_attn = (tokens[...].astype(jnp.float32) + projected).astype(jnp.bfloat16)
    second[...] = normed(after_attn, gain[...]).astype(jnp.bfloat16)
    seconds.start()
    seconds.arrive()
    weights.arrive()
    ffn = ffn_all[...].reshape(packed, 2048)
    gate_up = lax.dot_general(
        second_all[...].reshape(2 * GROUP, 2048),
        ffn,
        (((1,), (1,)), ((), ())),
        preferred_element_type=jnp.float32,
    )
    upward = pltpu.roll(gate_up, packed - 5, 1)
    hidden = pltpu.roll(gate_up / (1.0 + jnp.exp(-gate_up)) * upward, 10, 1)
    lane = lax.rem(lax.broadcasted_iota(jnp.int32, hidden.shape, 1), TILE)
    hidden = jnp.where((lane >= 10) & (lane < 15), hidden, 0.0).astype(jnp.bfloat16)
    product = jnp.dot(hidden, ffn, preferred_element_type=jnp.float32)
    down[...] = product.astype(jnp.bfloat16).reshape(GROUP, 2, 2048)
    downs.start()
    downs.arrive()
    total = jnp.sum(down_all[...].astype(jnp.float32), axis=0)
    out_ref[...] = (after_attn.astype(jnp.float32) + total).astype(jnp.bfloat16)
    for transfer in (rows, weights, parts, seconds, downs):
        transfer.sent()


def call(kernel, name, ident, outs, scratch, transfers, arrays):
    n_out = len(outs)
    vmem = pl.BlockSpec(memory_space=pltpu.VMEM)
    return pl.pallas_call(
        kernel,
        name=name,
        out_shape=outs,
        in_specs=[vmem] * len(arrays),
        out_specs=[vmem] * n_out,
        scratch_shapes=[pltpu.VMEM(shape, jnp.bfloat16) for shape in scratch]
        + [pltpu.SemaphoreType.DMA((transfers,))] * 3,
        compiler_params=pltpu.CompilerParams(collective_id=ident, has_side_effects=True),
    )(*arrays)


def normed(values, gain):
    wide = values.astype(jnp.float32)
    return wide * lax.rsqrt(jnp.mean(wide * wide, axis=-1, keepdims=True) + 1e-05) * gain


def rotate(tensor, cosine, sine):
    half = tensor.shape[-1] // 2
    first = tensor[..., :half]
    second = tensor[..., half:]
    return jnp.concatenate(
        [first * cosine - second * sine, second * cosine + first * sine], axis=-1
    )


def attend(queries, cache, visible, key_new, value_new):
    batch = queries.shape[0]
    n_key = KVH * HD
    same = (jnp.arange(H)[:, None] // (H // KVH) == jnp.arange(KVH)[None, :])[None, :, :, None]
    spread = jnp.where(same, queries[:, :, None, :], 0).reshape(batch, H, n_key)
    factor = HD ** (-0.5)
    scores = (
        jnp.einsum("rhe,rce->rhc", spread, cache[..., :n_key], preferred_element_type=jnp.float32)
        * factor
    )
    own_score = (
        jnp.sum(spread.astype(jnp.float32) * key_new.reshape(batch, 1, n_key).astype(jnp.float32), axis=-1)
        * factor
    )
    scores = jnp.where(visible[:, None, :], scores, -jnp.inf)
    peak = jnp.maximum(jnp.max(scores, axis=-1), own_score)
    weights = jnp.exp(scores - peak[..., None])
    own_weight = jnp.exp(own_score - peak)
    denom = jnp.sum(weights, axis=-1) + own_weight
    probs = (weights / denom[..., None]).astype(jnp.bfloat16)
    own_prob = (own_weight / denom).astype(jnp.bfloat16)
    mixed = jnp.einsum("rhc,rce->rhe", probs, cache[..., n_key:], preferred_element_type=jnp.float32)
    mixed = mixed + own_prob.astype(jnp.float32)[..., None] * value_new.reshape(
        batch, 1, n_key
    ).astype(jnp.float32)
    mixed = jnp.sum(jnp.where(same, mixed.reshape(batch, H, KVH, HD), 0.0), axis=2)
    return mixed.reshape(batch, H * HD).astype(jnp.bfloat16)


def scatter_columns(rows, depth):
    quads = GROUP // 4
    cut = rows.reshape(2, SHARDS, quads, depth)
    cut = jnp.pad(cut, ((0, 0), (0, 0), (0, 0), (0, TILE - depth)))
    return cut.transpose(2, 0, 1, 3).reshape(quads, 2, SHARDS * TILE)


def body(tokens, cache_lengths, kv_cache, attn_gain, mlp_gain, w_qkv, w_out, w_gate, w_up, w_down):
    n_query = H * HD
    n_key = KVH * HD
    packed = SHARDS * TILE
    w_attn = jnp.concatenate(
        [jnp.pad(w_qkv[0], ((0, 0), (0, 32))), jnp.pad(w_out[0], ((0, 6), (0, 0)))], axis=1
    )
    w_ffn = jnp.concatenate(
        [w_gate[0].T, w_up[0].T, w_down[0], jnp.zeros((1, w_down.shape[2]), w_down.dtype)], axis=0
    )

    normed_rows = normed(tokens, attn_gain[0]).astype(jnp.bfloat16)
    joint, attn_all = call(
        head_kernel,
        "head",
        0,
        [
            jax.ShapeDtypeStruct((4, 2, 512), jnp.float32),
            jax.ShapeDtypeStruct((SHARDS, TILE, 1024), jnp.bfloat16),
        ],
        [(GROUP, 2, packed), (GROUP, 2, 512), (GROUP, 2, 512)],
        3,
        [scatter_columns(normed_rows, 16), w_attn],
    )
    joint = joint[..., :480].transpose(1, 0, 2).reshape(2, 1920)

    freqs = jnp.exp(
        jnp.arange(HD // 2, dtype=jnp.float32) * (-2.0 * math.log(10000.0) / HD)
    )
    angles = cache_lengths.astype(jnp.float32)[:, None] * freqs[None, :]
    cosine = jnp.cos(angles)[:, None, :]
    sine = jnp.sin(angles)[:, None, :]
    turned = rotate(
        joint[:, : n_query + n_key].reshape(2, H + KVH, HD), cosine, sine
    ).astype(jnp.bfloat16)
    queries, key_new = turned[:, :H], turned[:, H:]
    value_new = joint[:, n_query + n_key :].astype(jnp.bfloat16)
    fresh = jnp.concatenate([key_new.reshape(2, n_key), value_new], axis=1)
    lengths_col = cache_lengths[:, None]
    positions = jnp.arange(CAP, dtype=jnp.int32)[None, :]
    visible = (positions < lengths_col) & (
        (positions < SINKS) | (positions > lengths_col - W)
    )
    context = attend(queries, kv_cache[0], visible, key_new, value_new)

    (stream,) = call(
        tail_kernel,
        "tail",
        1,
        [jax.ShapeDtypeStruct((2, 2048), jnp.bfloat16)],
        [
            (GROUP, 2, packed),
            (GROUP, 2, 512),
            (GROUP, 2, 512),
            (2, 2048),
            (GROUP, 2, 2048),
            (GROUP, 2, 2048),
            (GROUP, 2, 2048),
            (SHARDS, TILE, 2048),
        ],
        5,
        [scatter_columns(context, 10), attn_all, w_ffn, tokens, mlp_gain],
    )
    return (stream, fresh[None])


def solution(mesh):
    return jax.shard_map(
        body,
        mesh=mesh,
        in_specs=(
            P(("req", "fsdp"), None),
            P(("req", "fsdp")),
            P(None, ("req", "fsdp"), None, None),
            P(),
            P(),
            P(None, "req", "fsdp"),
            P(None, "req", "fsdp"),
            P(None, None, ("req", "fsdp")),
            P(None, None, ("req", "fsdp")),
            P(None, ("req", "fsdp"), None),
        ),
        out_specs=(P(("req", "fsdp"), None), P(None, ("req", "fsdp"), None)),
        check_vma=False,
    )
```

time: 152 us -> 103 us (0.68)
  Pallas kernels: 122 us -> 86.5 us
  other arithmetic: 12.3 us -> 6.3 us
  matrix products: 5.9 us -> 0.78 us
  local copies, waits for them, and re-layouts: 9.91 us -> 7.39 us
    pallas_call x6 -> x2, Pallas kernels: 122 us -> 86.5 us  [call(): pl.pallas_call(kernel, name=name, out_shape=outs, in_specs=[vmem] * len(a...]
    reduce_sum x3 -> x0, other arithmetic: 3.57 us -> none  [the longest x2 2.08 us: summed(): jnp.sum(parts.reshape(GROUP // 4, 4, 2, parts.shape[-1]), axis=0)]
    dot_general x4 -> x0, matrix products: 2.67 us -> none  [the longest x1 1.09 us: body(): jnp.dot(h_all.reshape(rows, packed), attn_all[:, :512], preferred_element...]
    reshape x3 -> x1, local copies, waits for them, and re-layouts: 2.47 us -> 0.1 us  [body(): joint = joint[..., :480].transpose(1, 0, 2).reshape(2, 1920)]
    dot_general x2 -> x0, local copies, waits for them, and re-layouts: 1.79 us -> none  [the longest x1 0.9 us: body(): jnp.dot(h_all.reshape(rows, packed), attn_all[:, :512], preferred_element...]
    unnamed x13 -> x10, local copies, waits for them, and re-layouts: 2.47 us -> 4.01 us
where the time goes in v2:
time: 103 us; the launch traced here: 102 us
  Pallas kernels  86.5 us (84%)
  local copies, waits for them, and re-layouts  7.39 us (7%)
  other arithmetic  6.3 us (6%)
    pallas_call x2, Pallas kernels, call(): pl.pallas_call(kernel, name=name, out_shape=outs, in_specs=[vmem] * len(a...  86.5 us
    unnamed x10, local copies, waits for them, and re-layouts  4.01 us

profile of v2, /device:TPU:1, one launch (start us, length us, event | category | flops | bytes accessed | tf_op | source)
XLA Modules:
  0.0 101.8 jit_solution(8935345812187625643)
XLA Ops:
  0.6 0.8 fusion.10
  1.5 0.8 fusion.12
  2.3 0.1 reshape.241
  2.4 0.7 reshape.242.h_ref
  3.1 1.3 %fusion.9.w_ref = bf16[16,1024]{1,0:T(8,128)(2,1)} fusion(bf16[10,512]{1,0:T(8,128)(2,1)} %bitcast.35, bf16[16,480]{1,0:T(8,128)(2,1)} %bitcast.36), kind=kLoop, calls=%fused_computation.21 | loop fusion | flops 131072 | bytes 58368 | tf_op jit(solution)/shard_map/concatenate | solution.py:248
  4.4 34.4 %head.1 = (f32[4,2,512]{2,1,0:T(2,128)}, bf16[8,16,1024]{2,1,0:T(8,128)(2,1)}) custom-call(bf16[16,2,128]{2,1,0:T(2,128)(2,1)} %reshape.242.h_ref, bf16[16,1024]{1,0:T(8,128)(2,1)} %fusion.9.w_ref), custom_call_target="tpu_custom_call" | custom-call | tf_op jit(solution)/shard_map/head/pallas_call | solution.py:182
  38.9 0.7 slice_bitcast_fusion
  39.6 0.1 reshape.243
  39.7 0.1 reshape.244
  39.8 0.7 fusion.18
  40.6 0.1 multiply_cosine_fusion
  40.7 0.1 add_convert_fusion
  40.8 0.1 fusion.13
  40.9 0.1 fusion.17
  41.0 0.2 multiply_reduce_fusion
  41.3 0.1 copy.37
  41.4 0.1 broadcast_in_dim.81
  41.5 0.1 broadcast_in_dim.77
  41.6 0.1 broadcast_in_dim.78
  41.7 2.7 %copy.35 = bf16[1,2,768,640]{2,3,1,0:T(8,128)(2,1)S(1)} copy(bf16[1,2,768,640]{3,2,1,0:T(8,128)(2,1)} %param.12) | data formatting | bytes 3932160 | tf_op args[2]
  44.6 0.3 fusion.19
  44.9 0.2 fusion.3
  45.2 0.4 convolution_add_fusion
  45.7 0.1 reshape.245
  45.8 0.2 select_reduce_fusion
  46.0 0.2 convert_element_type.69
  46.2 0.7 reshape.246.ctx_ref
  47.0 0.7 maximum_maximum_fusion.w_ffn
  47.7 52.1 %tail.1 = bf16[2,2048]{1,0:T(2,128)(2,1)} custom-call(bf16[16,2,128]{2,1,0:T(2,128)(2,1)} %reshape.246.ctx_ref, bf16[8,16,1024]{2,1,0:T(8,128)(2,1)} %get-tuple-element.5.w_out, bf16[16,2048]{1,0:T(8,128)(2,1)} %maximum_maximum_fusion.w_ffn, bf16[2,2048]{1,0:T(2,128)(2,1)} %tokens.1, f32[1,2048]{1,0:T(1,128)} %gain.1), custom_call_target="tpu_custom_call" | custom-call | tf_op jit(solution)/shard_map/tail/pallas_call | solution.py:182
  99.8 0.1 reshape.247
  99.9 0.7 maximum_bitcast_fusion
  100.5 1.3 %copy.48 = bf16[2,2048]{1,0:T(2,128)(2,1)} copy(bf16[2,2048]{1,0:T(2,128)(2,1)} %tail.1) | data formatting | bytes 16384
  (28 shorter events, 0.6 us)
Async XLA Ops:
  41.7 2.7 %copy-start.3 = (s32[2]{0:T(128)S(1)}, s32[2]{0:T(128)}, u32[]{:S(2)}) copy-start(s32[2]{0:T(128)} %param.11) | copy-start | bytes 28
  44.5 2.4 %copy-start = (bf16[1,5,2048]{2,1,0:T(8,128)(2,1)S(1)}, bf16[1,5,2048]{2,1,0:T(8,128)(2,1)}, u32[]{:S(2)}) copy-start(bf16[1,5,2048]{2,1,0:T(8,128)(2,1)} %param.19) | copy-start | bytes 61444
  44.5 2.4 %copy-start.1 = (bf16[1,2048,5]{1,2,0:T(8,128)(2,1)S(1)}, bf16[1,2048,5]{1,2,0:T(8,128)(2,1)}, u32[]{:S(2)}) copy-start(bf16[1,2048,5]{1,2,0:T(8,128)(2,1)} %param.18) | copy-start | bytes 61444
  44.6 2.4 %copy-start.2 = (bf16[1,2048,5]{1,2,0:T(8,128)(2,1)S(1)}, bf16[1,2048,5]{1,2,0:T(8,128)(2,1)}, u32[]{:S(2)}) copy-start(bf16[1,2048,5]{1,2,0:T(8,128)(2,1)} %param.17) | copy-start | bytes 61444

commit v3 on v2

v3 whole, which is shorter than its diff:
```python
import math

import jax
import jax.numpy as jnp
from jax import lax
from jax.experimental import pallas as pl
from jax.experimental.pallas import tpu as pltpu
from jax.sharding import PartitionSpec as P

H = 20
KVH = 5
HD = 64
CAP = 768
W = 384
SINKS = 4
DEVICES = 512
GROUP = 64
SHARDS = DEVICES // GROUP
TILE = 16
MESH = pl.DeviceIdType.MESH


def device(flat):
    return (lax.div(flat, 4), lax.rem(flat, 4))


def place():
    flat = lax.axis_index("req") * 4 + lax.axis_index("fsdp")
    return lax.rem(flat, GROUP), lax.div(flat, GROUP)


def group_peer(member, shard, i):
    peer = lax.rem(member + i, GROUP)
    return peer, device(shard * GROUP + peer)


def shard_peer(member, shard, i):
    return device(lax.rem(shard + i, SHARDS) * GROUP + member)


def greet(member, shard):
    barrier = pltpu.get_barrier_semaphore()

    def in_group(i, c):
        pl.semaphore_signal(
            barrier, inc=1, device_id=group_peer(member, shard, i)[1], device_id_type=MESH
        )
        return c

    def in_shards(i, c):
        pl.semaphore_signal(
            barrier, inc=1, device_id=shard_peer(member, shard, i), device_id_type=MESH
        )
        return c

    lax.fori_loop(1, GROUP, in_group, 0)
    lax.fori_loop(1, SHARDS, in_shards, 0)
    return barrier


class Transfer:
    def __init__(self, pick, dst, sems, k, member, shard, shards=False):
        self.pick, self.dst, self.member, self.shard, self.shards = pick, dst, member, shard, shards
        self.send, self.recv, self.own = (s.at[k] for s in sems)

    def local(self):
        mine = self.shard if self.shards else self.member
        return pltpu.make_async_copy(self.pick(self.member), self.dst.at[mine], self.own)

    def start(self):
        def step(i, c):
            if self.shards:
                peer, slot, target = i, self.shard, shard_peer(self.member, self.shard, i)
            else:
                peer, target = group_peer(self.member, self.shard, i)
                slot = self.member
            pltpu.make_async_remote_copy(
                src_ref=self.pick(peer),
                dst_ref=self.dst.at[slot],
                send_sem=self.send,
                recv_sem=self.recv,
                device_id=target,
                device_id_type=MESH,
            ).start()
            return c

        lax.fori_loop(1, SHARDS if self.shards else GROUP, step, 0)
        self.local().start()

    def arrive(self):
        others = self.dst.at[pl.ds(0, (SHARDS if self.shards else GROUP) - 1)]
        self.local().wait()
        pltpu.make_async_copy(others, others, self.recv).wait()

    def sent(self):
        others = self.dst.at[pl.ds(0, (SHARDS if self.shards else GROUP) - 1)]
        pltpu.make_async_copy(others, others, self.send).wait()


def iota(shape, axis):
    return lax.broadcasted_iota(jnp.int32, shape, axis)


def normed(values, gain):
    wide = values.astype(jnp.float32)
    return wide * lax.rsqrt(jnp.mean(wide * wide, axis=-1, keepdims=True) + 1e-05) * gain


def scatter_rows(rows, out):
    lane = lax.shift_right_logical(iota((2, 128), 1), 4)
    for quad in range(GROUP // 4):
        total = jnp.zeros((2, 128), jnp.float32)
        for s in range(SHARDS):
            block = 2 * s + quad // 8
            piece = rows[:, block * 128 : (block + 1) * 128]
            shift = (16 * (s - quad % 8)) % 128
            if shift:
                piece = pltpu.roll(piece, shift, 1)
            total = jnp.where(lane == s, piece, total)
        out[quad] = total.astype(jnp.bfloat16)


def head_key(column):
    return lax.shift_right_logical(column, 8) * 64 + (column & 63)


def context_column(t):
    low = t & 15
    column = 160 * (lax.shift_right_logical(t, 4) & 7) + 10 * lax.shift_right_logical(t, 7) + low
    return column, low < 10


def cache_key():
    entry = iota((1, 2 * KVH * HD), 1)
    return jnp.where(entry < KVH * HD, entry, entry - KVH * HD)


def attend(qkv, row, kv, seen, spread, gather):
    n_key = KVH * HD
    heads = 32
    queries = qkv[row : row + 1, : H * HD].astype(jnp.float32)
    fresh = qkv[row : row + 1, H * HD :].astype(jnp.float32)
    lane_head = lax.shift_right_logical(iota((heads, H * HD), 1), 6)
    wide = jnp.where(lane_head == iota((heads, H * HD), 0), queries, 0.0).astype(jnp.bfloat16)
    wide = jnp.dot(wide, spread, preferred_element_type=jnp.float32)
    entry = iota((heads, 2 * n_key), 1)
    wide = jnp.where(entry < n_key, wide, 0.0)
    factor = HD ** (-0.5)
    scores = factor * lax.dot_general(
        wide.astype(jnp.bfloat16),
        kv,
        (((1,), (1,)), ((), ())),
        preferred_element_type=jnp.float32,
    )
    own_score = factor * jnp.sum(wide * fresh, axis=-1, keepdims=True)
    scores = jnp.where(seen > 0, scores, -jnp.inf)
    peak = jnp.maximum(jnp.max(scores, axis=-1, keepdims=True), own_score)
    weights = jnp.exp(scores - peak)
    own_weight = jnp.exp(own_score - peak)
    denom = jnp.sum(weights, axis=-1, keepdims=True) + own_weight
    probs = (weights / denom).astype(jnp.bfloat16)
    own_prob = (own_weight / denom).astype(jnp.bfloat16).astype(jnp.float32)
    mixed = jnp.dot(probs, kv, preferred_element_type=jnp.float32) + own_prob * fresh
    kv_head = lax.shift_right_logical(entry, 6) - KVH
    own_head = lax.shift_right_logical(iota((heads, 2 * n_key), 0), 2)
    mixed = jnp.where(kv_head == own_head, mixed, 0.0).astype(jnp.bfloat16)
    moved = lax.dot_general(
        mixed, gather, (((1,), (1,)), ((), ())), preferred_element_type=jnp.float32
    )
    column, _ = context_column(iota(moved.shape, 1))
    moved = jnp.where(lax.shift_right_logical(column, 6) == iota(moved.shape, 0), moved, 0.0)
    return jnp.sum(moved, axis=0, keepdims=True)


def layer_kernel(
    tokens, attn_gain, mlp_gain, w_attn, w_ffn, cosine, sine, seen, cache,
    out_ref, fresh_ref,
    kv, h_src, h_all, attn_all, qkv_part, qkv_all, ctx_src, ctx_all, out_part, out_all,
    second, second_all, down, down_all, ffn_all, spread, gather, joint, kv_sem, *sems
):
    member, shard = place()
    packed = SHARDS * TILE
    load = pltpu.make_async_copy(cache, kv, kv_sem.at[0])
    load.start()
    barrier = greet(member, shard)
    scatter_rows(normed(tokens[...], attn_gain[...]), h_src)
    spread[...] = (head_key(iota((H * HD, 1), 0)) == cache_key()).astype(jnp.float32).astype(
        jnp.bfloat16
    )
    column, real = context_column(iota((GROUP // 4 * packed, 1), 0))
    gather[...] = (
        (jnp.where(real, head_key(column), -1) == cache_key())
        .astype(jnp.float32)
        .astype(jnp.bfloat16)
    )
    attn_weights = Transfer(lambda peer: w_attn, attn_all, sems, 0, member, shard, shards=True)
    rows = Transfer(lambda peer: h_src.at[lax.div(peer, 4)], h_all, sems, 1, member, shard)
    ffn_weights = Transfer(lambda peer: w_ffn, ffn_all, sems, 2, member, shard, shards=True)
    qkvs = Transfer(lambda peer: qkv_part.at[peer], qkv_all, sems, 3, member, shard)
    contexts = Transfer(lambda peer: ctx_src.at[lax.div(peer, 4)], ctx_all, sems, 4, member, shard)
    outs = Transfer(lambda peer: out_part.at[peer], out_all, sems, 5, member, shard)
    seconds = Transfer(lambda peer: second, second_all, sems, 6, member, shard)
    downs = Transfer(lambda peer: down.at[peer], down_all, sems, 7, member, shard)

    pl.semaphore_wait(barrier, GROUP + SHARDS - 2)
    rows.start()
    attn_weights.start()
    rows.arrive()
    attn_weights.arrive()
    product = jnp.dot(
        h_all[...].reshape(2 * GROUP, packed),
        attn_all[...].reshape(packed, 1024)[:, :512],
        preferred_element_type=jnp.float32,
    )
    qkv_part[...] = product.astype(jnp.bfloat16).reshape(GROUP, 2, 512)
    qkvs.start()
    ffn_weights.start()
    qkvs.arrive()
    summed = jnp.sum(
        qkv_all[...].astype(jnp.float32).reshape(GROUP // 4, 4, 2, 512), axis=0
    )
    for x in range(4):
        joint[:, 480 * x : 480 * (x + 1)] = summed[x][:, :480]
    straight = joint[...]
    width = straight.shape[1]
    lane = iota(straight.shape, 1)
    partner = jnp.where(
        (lane & 63) < 32, pltpu.roll(straight, width - 32, 1), pltpu.roll(straight, 32, 1)
    )
    turned = straight * jnp.concatenate([cosine[...]] * 15, axis=-1) + partner * jnp.concatenate(
        [sine[...]] * 15, axis=-1
    )
    qkv = jnp.where(lane < (H + KVH) * HD, turned, straight).astype(jnp.bfloat16)
    fresh_ref[...] = qkv[:, H * HD :]
    load.wait()
    context = [
        attend(qkv, r, kv[r], seen[r : r + 1, :], spread[...], gather[...]) for r in range(2)
    ]
    context = jnp.concatenate(context, axis=0).astype(jnp.bfloat16)
    for quad in range(GROUP // 4):
        ctx_src[quad] = context[:, quad * packed : (quad + 1) * packed]
    contexts.start()
    contexts.arrive()
    product = jnp.dot(
        ctx_all[...].reshape(2 * GROUP, packed),
        attn_all[...].reshape(packed, 1024)[:, 512:],
        preferred_element_type=jnp.float32,
    )
    out_part[...] = product.astype(jnp.bfloat16).reshape(GROUP, 2, 512)
    outs.start()
    outs.arrive()
    projected = jnp.sum(
        out_all[...].astype(jnp.float32).reshape(GROUP // 4, 4, 2, 512), axis=0
    )
    projected = jnp.concatenate([projected[x] for x in range(4)], axis=-1)
    after_attn = (tokens[...].astype(jnp.float32) + projected).astype(jnp.bfloat16)
    second[...] = normed(after_attn, mlp_gain[...]).astype(jnp.bfloat16)
    seconds.start()
    seconds.arrive()
    ffn_weights.arrive()
    ffn = ffn_all[...].reshape(packed, 2048)
    gate_up = lax.dot_general(
        second_all[...].reshape(2 * GROUP, 2048),
        ffn,
        (((1,), (1,)), ((), ())),
        preferred_element_type=jnp.float32,
    )
    upward = pltpu.roll(gate_up, packed - 5, 1)
    hidden = pltpu.roll(gate_up / (1.0 + jnp.exp(-gate_up)) * upward, 10, 1)
    lane = iota(hidden.shape, 1) & (TILE - 1)
    hidden = jnp.where((lane >= 10) & (lane < 15), hidden, 0.0).astype(jnp.bfloat16)
    product = jnp.dot(hidden, ffn, preferred_element_type=jnp.float32)
    down[...] = product.astype(jnp.bfloat16).reshape(GROUP, 2, 2048)
    downs.start()
    downs.arrive()
    total = jnp.sum(down_all[...].astype(jnp.float32), axis=0)
    out_ref[...] = (after_attn.astype(jnp.float32) + total).astype(jnp.bfloat16)
    for transfer in (attn_weights, rows, ffn_weights, qkvs, contexts, outs, seconds, downs):
        transfer.sent()


def body(tokens, cache_lengths, kv_cache, attn_gain, mlp_gain, w_qkv, w_out, w_gate, w_up, w_down):
    packed = SHARDS * TILE
    w_attn = jnp.concatenate(
        [jnp.pad(w_qkv[0], ((0, 0), (0, 32))), jnp.pad(w_out[0], ((0, 6), (0, 0)))], axis=1
    )
    w_ffn = jnp.concatenate(
        [w_gate[0].T, w_up[0].T, w_down[0], jnp.zeros((1, w_down.shape[2]), w_down.dtype)], axis=0
    )
    lane = jnp.arange(128)
    freqs = jnp.exp((lane % 32).astype(jnp.float32) * (-2.0 * math.log(10000.0) / HD))
    angles = cache_lengths.astype(jnp.float32)[:, None] * freqs[None, :]
    cosine = jnp.cos(angles)
    sine = jnp.sin(angles) * jnp.where(lane % 64 < 32, -1.0, 1.0)
    lengths_col = cache_lengths[:, None]
    positions = jnp.arange(CAP, dtype=jnp.int32)[None, :]
    visible = (positions < lengths_col) & (
        (positions < SINKS) | (positions > lengths_col - W)
    )
    vmem = pl.BlockSpec(memory_space=pltpu.VMEM)
    transfers = 8
    shapes = [
        (2, CAP, 640),
        (GROUP // 4, 2, packed),
        (GROUP, 2, packed),
        (SHARDS, TILE, 1024),
        (GROUP, 2, 512),
        (GROUP, 2, 512),
        (GROUP // 4, 2, packed),
        (GROUP, 2, packed),
        (GROUP, 2, 512),
        (GROUP, 2, 512),
        (2, 2048),
        (GROUP, 2, 2048),
        (GROUP, 2, 2048),
        (GROUP, 2, 2048),
        (SHARDS, TILE, 2048),
        (H * HD, 640),
        (GROUP // 4 * packed, 640),
    ]
    stream, fresh = pl.pallas_call(
        layer_kernel,
        name="layer",
        out_shape=[
            jax.ShapeDtypeStruct((2, 2048), jnp.bfloat16),
            jax.ShapeDtypeStruct((2, 640), jnp.bfloat16),
        ],
        in_specs=[vmem] * 8 + [pl.BlockSpec(memory_space=pl.ANY)],
        out_specs=[vmem] * 2,
        scratch_shapes=[pltpu.VMEM(shape, jnp.bfloat16) for shape in shapes]
        + [pltpu.VMEM((2, 1920), jnp.float32), pltpu.SemaphoreType.DMA((1,))]
        + [pltpu.SemaphoreType.DMA((transfers,))] * 3,
        compiler_params=pltpu.CompilerParams(collective_id=0, has_side_effects=True),
    )(
        tokens,
        attn_gain,
        mlp_gain,
        w_attn,
        w_ffn,
        cosine,
        sine,
        visible.astype(jnp.float32),
        kv_cache[0],
    )
    return (stream, fresh[None])


def solution(mesh):
    return jax.shard_map(
        body,
        mesh=mesh,
        in_specs=(
            P(("req", "fsdp"), None),
            P(("req", "fsdp")),
            P(None, ("req", "fsdp"), None, None),
            P(),
            P(),
            P(None, "req", "fsdp"),
            P(None, "req", "fsdp"),
            P(None, None, ("req", "fsdp")),
            P(None, None, ("req", "fsdp")),
            P(None, ("req", "fsdp"), None),
        ),
        out_specs=(P(("req", "fsdp"), None), P(None, ("req", "fsdp"), None)),
        check_vma=False,
    )
```

time: 103 us -> 93 us (0.903)
  local copies, waits for them, and re-layouts: 7.39 us -> 2.64 us
  Pallas kernels: 86.5 us -> 83.7 us
    pallas_call x2 -> x1, Pallas kernels: 86.5 us -> 83.7 us  [body(): pl.pallas_call(layer_kernel, name='layer', out_shape=[jax.ShapeDtypeStruc...]
    reshape x8 -> x0, local copies, waits for them, and re-layouts: 1.91 us -> none  [the longest x2 1.41 us: scatter_columns(): return cut.transpose(2, 0, 1, 3).reshape(quads, 2, SHARDS * TILE)]
    unnamed x10 -> x2, local copies, waits for them, and re-layouts: 4.01 us -> 2.56 us
    reduce_sum x4 -> x0, other arithmetic: 1.39 us -> none  [the longest x1 0.83 us: normed(): jnp.mean(wide * wide, axis=-1, keepdims=True) + 1e-05]
where the time goes in v3:
time: 93 us; the launch traced here: 92.6 us
  Pallas kernels  83.7 us (90%)
  other arithmetic  5.58 us (6%)
  local copies, waits for them, and re-layouts  2.64 us (3%)
    pallas_call x1, Pallas kernels, body(): pl.pallas_call(layer_kernel, name='layer', out_shape=[jax.ShapeDtypeStruc...  83.7 us
    unnamed x2, local copies, waits for them, and re-layouts  2.56 us

profile of v3, /device:TPU:1, one launch (start us, length us, event | category | flops | bytes accessed | tf_op | source)
XLA Modules:
  0.0 92.6 jit_solution(2201674357251628585)
XLA Ops:
  0.6 0.1 pad.13.clone
  0.7 0.7 broadcast_add_fusion
  1.5 0.7 fusion.3
  2.1 1.3 %and_convert_fusion.seen = f32[2,768]{1,0:T(2,128)} fusion(pred[768]{0:T(1024)(128)(4,1)S(1)} %iota_compare_fusion.2, s32[2]{0:T(128)S(1)} %get-tuple-element.8, s32[2]{0:T(128)} %param.11), kind=kLoop, calls=%fused_computation.6 | loop fusion | flops 7680 | bytes 6928 | tf_op jit(solution)/shard_map/convert_element_type | solution.py:342
  3.5 1.3 %fusion.2.w_attn = bf16[16,1024]{1,0:T(8,128)(2,1)} fusion(bf16[10,512]{1,0:T(8,128)(2,1)} %bitcast.16, bf16[16,480]{1,0:T(8,128)(2,1)} %bitcast.17), kind=kLoop, calls=%fused_computation.5 | loop fusion | flops 131072 | bytes 58368 | tf_op jit(solution)/shard_map/concatenate | solution.py:284
  4.8 1.5 %maximum_maximum_fusion.w_ffn = bf16[16,2048]{1,0:T(8,128)(2,1)} fusion(bf16[5,2048]{1,0:T(8,128)(2,1)} %bitcast.13, bf16[5,2048]{1,0:T(8,128)(2,1)} %bitcast.14, bf16[5,2048]{1,0:T(8,128)(2,1)} %bitcast.15, bf16[16]{0:T(256)(128)(2,1)S(1)} %pad.13.clone), kind=kLoop, calls=%fused_computation.2 | loop fusion | flops 262144 | bytes 127008 | tf_op jit(solution)/shard_map/concatenate | solution.py:287
  6.3 83.7 %layer.1 = (bf16[2,2048]{1,0:T(2,128)(2,1)}, bf16[2,640]{1,0:T(2,128)(2,1)}) custom-call(bf16[2,2048]{1,0:T(2,128)(2,1)} %tokens.1, f32[1,2048]{1,0:T(1,128)} %attn_gain.1, f32[1,2048]{1,0:T(1,128)} %mlp_gain.1, bf16[16,1024]{1,0:T(8,128)(2,1)} %fusion.2.w_attn, bf16[16,2048]{1,0:T(8,128)(2,1)} %maximum_maximum_fusion.w_ffn, ...), custom_call_target="tpu_custom_call" | custom-call | tf_op jit(solution)/shard_map/layer/pallas_call | solution.py:321
  90.0 1.3 %copy.14 = bf16[2,2048]{1,0:T(2,128)(2,1)} copy(bf16[2,2048]{1,0:T(2,128)(2,1)} %get-tuple-element.14) | data formatting | bytes 16384
  91.3 1.3 %copy.15 = bf16[1,2,640]{2,1,0:T(2,128)(2,1)} copy(bf16[1,2,640]{2,1,0:T(2,128)(2,1)} %bitcast.18) | data formatting | bytes 5120
  (2 shorter events, 0.0 us)

commit v4 on v3

v4 whole, which is shorter than its diff:
```python
import math

import jax
import jax.numpy as jnp
from jax import lax
from jax.experimental import pallas as pl
from jax.experimental.pallas import tpu as pltpu
from jax.sharding import PartitionSpec as P

H = 20
KVH = 5
HD = 64
CAP = 768
W = 384
SINKS = 4
DEVICES = 512
GROUP = 32
QUADS = GROUP // 4
SHARDS = DEVICES // GROUP
TILE = 16
ROWS = SHARDS // 2
MESH = pl.DeviceIdType.MESH


def device(flat):
    return (lax.div(flat, 4), lax.rem(flat, 4))


def place():
    flat = lax.axis_index("req") * 4 + lax.axis_index("fsdp")
    return lax.rem(flat, GROUP), lax.div(flat, GROUP)


def group_peer(member, shard, i):
    peer = lax.rem(member + i, GROUP)
    return peer, device(shard * GROUP + peer)


def row_peer(member, shard, i):
    return device(lax.rem(shard + 2 * i, SHARDS) * GROUP + member)


def partner_of(member, shard):
    return device((shard + 1 - 2 * lax.rem(shard, 2)) * GROUP + member)


def greet(member, shard):
    barrier = pltpu.get_barrier_semaphore()

    def in_group(i, c):
        pl.semaphore_signal(
            barrier, inc=1, device_id=group_peer(member, shard, i)[1], device_id_type=MESH
        )
        return c

    def in_row(i, c):
        pl.semaphore_signal(
            barrier, inc=1, device_id=row_peer(member, shard, i), device_id_type=MESH
        )
        return c

    lax.fori_loop(1, GROUP, in_group, 0)
    lax.fori_loop(1, ROWS, in_row, 0)
    pl.semaphore_signal(
        barrier, inc=1, device_id=partner_of(member, shard), device_id_type=MESH
    )
    return barrier


class Transfer:
    def __init__(self, pick, dst, sems, k, member, shard):
        self.pick, self.dst, self.member, self.shard = pick, dst, member, shard
        self.send, self.recv, self.own = (s.at[k] for s in sems)
        self.others = dst.at[pl.ds(0, GROUP - 1)]

    def local(self):
        return pltpu.make_async_copy(
            self.pick(self.member), self.dst.at[self.member], self.own
        )

    def start(self):
        def step(i, c):
            peer, target = group_peer(self.member, self.shard, i)
            pltpu.make_async_remote_copy(
                src_ref=self.pick(peer),
                dst_ref=self.dst.at[self.member],
                send_sem=self.send,
                recv_sem=self.recv,
                device_id=target,
                device_id_type=MESH,
            ).start()
            return c

        lax.fori_loop(1, GROUP, step, 0)
        self.local().start()

    def arrive(self):
        self.local().wait()
        pltpu.make_async_copy(self.others, self.others, self.recv).wait()

    def sent(self):
        pltpu.make_async_copy(self.others, self.others, self.send).wait()


class Weights:
    def __init__(self, src, dst, sems, k, member, shard):
        self.src, self.dst, self.member, self.shard = src, dst, member, shard
        self.send, self.recv, self.own = (s.at[k] for s in sems)
        self.send_row, self.recv_row = (s.at[k + 1] for s in sems[:2])
        self.pair = dst.at[pl.ds(2 * lax.div(shard, 2), 2)]
        self.others = dst.at[pl.ds(0, SHARDS - 2)]

    def local(self):
        return pltpu.make_async_copy(self.src, self.dst.at[self.shard], self.own)

    def swap(self):
        return pltpu.make_async_remote_copy(
            src_ref=self.src,
            dst_ref=self.dst.at[self.shard],
            send_sem=self.send,
            recv_sem=self.recv,
            device_id=partner_of(self.member, self.shard),
            device_id_type=MESH,
        )

    def start(self):
        self.swap().start()
        self.local().start()

    def relay(self):
        self.local().wait()
        self.swap().wait()

        def step(i, c):
            pltpu.make_async_remote_copy(
                src_ref=self.pair,
                dst_ref=self.pair,
                send_sem=self.send_row,
                recv_sem=self.recv_row,
                device_id=row_peer(self.member, self.shard, i),
                device_id_type=MESH,
            ).start()
            return c

        lax.fori_loop(1, ROWS, step, 0)

    def arrive(self):
        pltpu.make_async_copy(self.others, self.others, self.recv_row).wait()

    def sent(self):
        pltpu.make_async_copy(self.others, self.others, self.send_row).wait()


def iota(shape, axis):
    return lax.broadcasted_iota(jnp.int32, shape, axis)


def normed(values, gain):
    wide = values.astype(jnp.float32)
    return wide * lax.rsqrt(jnp.mean(wide * wide, axis=-1, keepdims=True) + 1e-05) * gain


def scatter_rows(rows, out):
    lane = lax.shift_right_logical(iota((2, 128), 1), 4)
    for quad in range(QUADS):
        for half in range(2):
            total = jnp.zeros((2, 128), jnp.float32)
            for s in range(8):
                block = 8 * half + s
                piece = rows[:, block * 128 : (block + 1) * 128]
                shift = (16 * (s - quad)) % 128
                if shift:
                    piece = pltpu.roll(piece, shift, 1)
                total = jnp.where(lane == s, piece, total)
            out[quad, :, half * 128 : (half + 1) * 128] = total.astype(jnp.bfloat16)


def head_key(column):
    return lax.shift_right_logical(column, 8) * 64 + (column & 63)


def context_column(t):
    low = t & 15
    column = 80 * (lax.shift_right_logical(t, 4) & 15) + 10 * lax.shift_right_logical(t, 8) + low
    return column, low < 10


def cache_key():
    entry = iota((1, 2 * KVH * HD), 1)
    return jnp.where(entry < KVH * HD, entry, entry - KVH * HD)


def visible(position, length):
    return (position < length) & ((position < SINKS) | (position > length - W))


def attend(qkv, row, kv, seen, spread, gather):
    n_key = KVH * HD
    heads = 32
    queries = qkv[row : row + 1, : H * HD].astype(jnp.float32)
    fresh = qkv[row : row + 1, H * HD :].astype(jnp.float32)
    lane_head = lax.shift_right_logical(iota((heads, H * HD), 1), 6)
    wide = jnp.where(lane_head == iota((heads, H * HD), 0), queries, 0.0).astype(jnp.bfloat16)
    wide = jnp.dot(wide, spread, preferred_element_type=jnp.float32)
    entry = iota((heads, 2 * n_key), 1)
    wide = jnp.where(entry < n_key, wide, 0.0)
    factor = HD ** (-0.5)
    scores = factor * lax.dot_general(
        wide.astype(jnp.bfloat16),
        kv,
        (((1,), (1,)), ((), ())),
        preferred_element_type=jnp.float32,
    )
    own_score = factor * jnp.sum(wide * fresh, axis=-1, keepdims=True)
    scores = jnp.where(seen, scores, -jnp.inf)
    peak = jnp.maximum(jnp.max(scores, axis=-1, keepdims=True), own_score)
    weights = jnp.exp(scores - peak)
    own_weight = jnp.exp(own_score - peak)
    denom = jnp.sum(weights, axis=-1, keepdims=True) + own_weight
    probs = (weights / denom).astype(jnp.bfloat16)
    own_prob = (own_weight / denom).astype(jnp.bfloat16).astype(jnp.float32)
    mixed = jnp.dot(probs, kv, preferred_element_type=jnp.float32) + own_prob * fresh
    kv_head = lax.shift_right_logical(entry, 6) - KVH
    own_head = lax.shift_right_logical(iota((heads, 2 * n_key), 0), 2)
    mixed = jnp.where(kv_head == own_head, mixed, 0.0).astype(jnp.bfloat16)
    moved = lax.dot_general(
        mixed, gather, (((1,), (1,)), ((), ())), preferred_element_type=jnp.float32
    )
    column, _ = context_column(iota(moved.shape, 1))
    moved = jnp.where(lax.shift_right_logical(column, 6) == iota(moved.shape, 0), moved, 0.0)
    return jnp.sum(moved, axis=0, keepdims=True)


def layer_kernel(
    tokens, lengths, attn_gain, mlp_gain, w_qkv, w_out, w_gate, w_up, w_down, cache,
    out_ref,
    kv, h_src, h_all, qkv_src, wqkv_all, wout_src, wout_all, ffn_src, ffn_all,
    qkv_part, qkv_all, ctx_src, ctx_all, out_part, out_all,
    second, second_all, down, down_all, spread, gather, joint, kv_sem, *sems
):
    member, shard = place()
    packed = SHARDS * TILE
    load = pltpu.make_async_copy(cache, kv, kv_sem.at[0])
    load.start()
    barrier = greet(member, shard)
    qkv_src[...] = jnp.zeros_like(qkv_src)
    qkv_src[:, :480] = w_qkv[...]
    wout_src[...] = jnp.zeros_like(wout_src)
    wout_src[:10, :] = w_out[...]
    ffn_src[...] = jnp.concatenate(
        [w[...].astype(jnp.float32) for w in (w_gate, w_up, w_down)]
        + [jnp.zeros((1, 2048), jnp.float32)],
        axis=0,
    ).astype(jnp.bfloat16)
    scatter_rows(normed(tokens[...], attn_gain[...]), h_src)
    spread[...] = (head_key(iota((H * HD, 1), 0)) == cache_key()).astype(jnp.float32).astype(
        jnp.bfloat16
    )
    column, real = context_column(iota((QUADS * packed, 1), 0))
    gather[...] = (
        (jnp.where(real, head_key(column), -1) == cache_key())
        .astype(jnp.float32)
        .astype(jnp.bfloat16)
    )
    lane = iota((2, 128), 1)
    freqs = jnp.exp((lane & 31).astype(jnp.float32) * (-2.0 * math.log(10000.0) / HD))
    angles = jnp.where(iota((2, 128), 0) == 0, lengths[0], lengths[1]).astype(jnp.float32) * freqs
    cosine = jnp.cos(angles)
    sine = jnp.sin(angles) * jnp.where((lane & 63) < 32, -1.0, 1.0)
    position = iota((1, CAP), 1)
    qkv_weights = Weights(qkv_src, wqkv_all, sems, 0, member, shard)
    out_weights = Weights(wout_src, wout_all, sems, 2, member, shard)
    ffn_weights = Weights(ffn_src, ffn_all, sems, 4, member, shard)
    rows = Transfer(lambda peer: h_src.at[lax.div(peer, 4)], h_all, sems, 6, member, shard)
    qkvs = Transfer(lambda peer: qkv_part.at[peer], qkv_all, sems, 7, member, shard)
    contexts = Transfer(lambda peer: ctx_src.at[lax.div(peer, 4)], ctx_all, sems, 8, member, shard)
    outs = Transfer(lambda peer: out_part.at[peer], out_all, sems, 9, member, shard)
    seconds = Transfer(lambda peer: second, second_all, sems, 10, member, shard)
    downs = Transfer(lambda peer: down.at[peer], down_all, sems, 11, member, shard)

    pl.semaphore_wait(barrier, GROUP + ROWS - 1)
    qkv_weights.start()
    rows.start()
    out_weights.start()
    qkv_weights.relay()
    out_weights.relay()
    ffn_weights.start()
    rows.arrive()
    qkv_weights.arrive()
    product = jnp.dot(
        h_all[...].reshape(2 * GROUP, packed),
        wqkv_all[...].reshape(packed, 512),
        preferred_element_type=jnp.float32,
    )
    qkv_part[...] = product.astype(jnp.bfloat16).reshape(GROUP, 2, 512)
    qkvs.start()
    ffn_weights.relay()
    qkvs.arrive()
    summed = jnp.sum(
        qkv_all[...].astype(jnp.float32).reshape(QUADS, 4, 2, 512), axis=0
    )
    for x in range(4):
        joint[:, 480 * x : 480 * (x + 1)] = summed[x][:, :480]
    straight = joint[...]
    width = straight.shape[1]
    lane = iota(straight.shape, 1)
    partner = jnp.where(
        (lane & 63) < 32, pltpu.roll(straight, width - 32, 1), pltpu.roll(straight, 32, 1)
    )
    turned = straight * jnp.concatenate([cosine] * 15, axis=-1) + partner * jnp.concatenate(
        [sine] * 15, axis=-1
    )
    qkv = jnp.where(lane < (H + KVH) * HD, turned, straight).astype(jnp.bfloat16)
    out_ref[:, 2048:] = qkv[:, H * HD :].astype(jnp.float32)
    load.wait()
    context = [
        attend(qkv, r, kv[r], visible(position, lengths[r]), spread[...], gather[...])
        for r in range(2)
    ]
    context = jnp.concatenate(context, axis=0).astype(jnp.bfloat16)
    for quad in range(QUADS):
        ctx_src[quad] = context[:, quad * packed : (quad + 1) * packed]
    contexts.start()
    contexts.arrive()
    out_weights.arrive()
    product = jnp.dot(
        ctx_all[...].reshape(2 * GROUP, packed),
        wout_all[...].reshape(packed, 512),
        preferred_element_type=jnp.float32,
    )
    out_part[...] = product.astype(jnp.bfloat16).reshape(GROUP, 2, 512)
    outs.start()
    outs.arrive()
    projected = jnp.sum(
        out_all[...].astype(jnp.float32).reshape(QUADS, 4, 2, 512), axis=0
    )
    projected = jnp.concatenate([projected[x] for x in range(4)], axis=-1)
    after_attn = (tokens[...].astype(jnp.float32) + projected).astype(jnp.bfloat16)
    second[...] = normed(after_attn, mlp_gain[...]).astype(jnp.bfloat16)
    seconds.start()
    seconds.arrive()
    ffn_weights.arrive()
    ffn = ffn_all[...].reshape(packed, 2048)
    gate_up = lax.dot_general(
        second_all[...].reshape(2 * GROUP, 2048),
        ffn,
        (((1,), (1,)), ((), ())),
        preferred_element_type=jnp.float32,
    )
    upward = pltpu.roll(gate_up, packed - 5, 1)
    hidden = pltpu.roll(gate_up / (1.0 + jnp.exp(-gate_up)) * upward, 10, 1)
    lane = iota(hidden.shape, 1) & (TILE - 1)
    hidden = jnp.where((lane >= 10) & (lane < 15), hidden, 0.0).astype(jnp.bfloat16)
    product = jnp.dot(hidden, ffn, preferred_element_type=jnp.float32)
    down[...] = product.astype(jnp.bfloat16).reshape(GROUP, 2, 2048)
    downs.start()
    downs.arrive()
    total = jnp.sum(down_all[...].astype(jnp.float32), axis=0)
    stream = (after_attn.astype(jnp.float32) + total).astype(jnp.bfloat16)
    out_ref[:, :2048] = stream.astype(jnp.float32)
    for transfer in (qkv_weights, out_weights, ffn_weights, rows, qkvs, contexts, outs, seconds, downs):
        transfer.sent()


def body(tokens, cache_lengths, kv_cache, attn_gain, mlp_gain, w_qkv, w_out, w_gate, w_up, w_down):
    packed = SHARDS * TILE
    vmem = pl.BlockSpec(memory_space=pltpu.VMEM)
    transfers = 12
    shapes = [
        (2, CAP, 640),
        (QUADS, 2, packed),
        (GROUP, 2, packed),
        (TILE, 512),
        (SHARDS, TILE, 512),
        (TILE, 512),
        (SHARDS, TILE, 512),
        (TILE, 2048),
        (SHARDS, TILE, 2048),
        (GROUP, 2, 512),
        (GROUP, 2, 512),
        (QUADS, 2, packed),
        (GROUP, 2, packed),
        (GROUP, 2, 512),
        (GROUP, 2, 512),
        (2, 2048),
        (GROUP, 2, 2048),
        (GROUP, 2, 2048),
        (GROUP, 2, 2048),
        (H * HD, 640),
        (QUADS * packed, 640),
    ]
    joined = pl.pallas_call(
        layer_kernel,
        name="layer",
        out_shape=jax.ShapeDtypeStruct((2, 2688), jnp.float32),
        in_specs=[vmem, pl.BlockSpec(memory_space=pltpu.SMEM)]
        + [vmem] * 7
        + [pl.BlockSpec(memory_space=pl.ANY)],
        out_specs=vmem,
        scratch_shapes=[pltpu.VMEM(shape, jnp.bfloat16) for shape in shapes]
        + [pltpu.VMEM((2, 1920), jnp.float32), pltpu.SemaphoreType.DMA((1,))]
        + [pltpu.SemaphoreType.DMA((transfers,))] * 3,
        compiler_params=pltpu.CompilerParams(collective_id=0, has_side_effects=True),
    )(
        tokens,
        cache_lengths,
        attn_gain,
        mlp_gain,
        w_qkv[0],
        w_out[0],
        w_gate[0].T,
        w_up[0].T,
        w_down[0],
        kv_cache[0],
    )
    joined = joined.astype(jnp.bfloat16)
    return (joined[:, :2048], joined[None, :, 2048:])


def solution(mesh):
    return jax.shard_map(
        body,
        mesh=mesh,
        in_specs=(
            P(("req", "fsdp"), None),
            P(("req", "fsdp")),
            P(None, ("req", "fsdp"), None, None),
            P(),
            P(),
            P(None, "req", "fsdp"),
            P(None, "req", "fsdp"),
            P(None, None, ("req", "fsdp")),
            P(None, None, ("req", "fsdp")),
            P(None, ("req", "fsdp"), None),
        ),
        out_specs=(P(("req", "fsdp"), None), P(None, ("req", "fsdp"), None)),
        check_vma=False,
    )
```

time: 93 us -> 71.5 us (0.77)
  Pallas kernels: 83.7 us -> 68.7 us
  other arithmetic: 5.58 us -> 0.74 us
  local copies, waits for them, and re-layouts: 2.64 us -> 1.19 us
    pallas_call x1, Pallas kernels: 83.7 us -> 68.7 us  [body(): pl.pallas_call(layer_kernel, name='layer', out_shape=jax.ShapeDtypeStruct...]
    concatenate x2 -> x0, other arithmetic: 2.82 us -> none  [the longest x1 1.48 us: body(): jnp.concatenate([w_gate[0].T, w_up[0].T, w_down[0], jnp.zeros((1, w_down....]
    unnamed x2 -> x0, local copies, waits for them, and re-layouts: 2.56 us -> none
where the time goes in v4:
time: 71.5 us; the launch traced here: 71.2 us
  Pallas kernels  68.7 us (96%)
  local copies, waits for them, and re-layouts  1.19 us (2%)
  other arithmetic  0.74 us (1%)
    pallas_call x1, Pallas kernels, body(): pl.pallas_call(layer_kernel, name='layer', out_shape=jax.ShapeDtypeStruct...  68.7 us

profile of v4, /device:TPU:1, one launch (start us, length us, event | category | flops | bytes accessed | tf_op | source)
XLA Modules:
  0.0 71.2 jit_solution(4810291555712280889)
XLA Ops:
  0.6 68.7 %layer.1 = f32[2,2688]{1,0:T(2,128)} custom-call(bf16[2,2048]{1,0:T(2,128)(2,1)} %tokens.1, s32[2]{0:T(128)} %lengths.1, f32[1,2048]{1,0:T(1,128)} %attn_gain.1, f32[1,2048]{1,0:T(1,128)} %mlp_gain.1, bf16[16,480]{1,0:T(8,128)(2,1)} %bitcast.16, bf16[10,512]{1,0:T(8,128)(2,1)} %bitcast.17, bf16[5,2048]{1,0:T(8,128)(2,1)} %bitcast.13, ...), custom_call_target="tpu_custom_call" | custom-call | tf_op jit(solution)/shard_map/layer/pallas_call | solution.py:392
  69.3 0.7 %convert_element_type.3 = bf16[2,2688]{1,0:T(2,128)(2,1)S(1)} convert(f32[2,2688]{1,0:T(2,128)} %layer.1) | non-fusion elementwise | flops 5376 | bytes 32256 | tf_op jit(solution)/shard_map/convert_element_type | solution.py:416
  70.1 0.6 slice_bitcast_fusion
  70.6 0.6 slice.8

commit v5 on v4

--- a/solution.py
+++ b/solution.py
@@ -107,7 +107,7 @@
         self.src, self.dst, self.member, self.shard = src, dst, member, shard
         self.send, self.recv, self.own = (s.at[k] for s in sems)
         self.send_row, self.recv_row = (s.at[k + 1] for s in sems[:2])
-        self.pair = dst.at[pl.ds(2 * lax.div(shard, 2), 2)]
+        self.partner = shard + 1 - 2 * lax.rem(shard, 2)
         self.others = dst.at[pl.ds(0, SHARDS - 2)]
 
     def local(self):
@@ -123,18 +123,11 @@
             device_id_type=MESH,
         )
 
-    def start(self):
-        self.swap().start()
-        self.local().start()
-
-    def relay(self):
-        self.local().wait()
-        self.swap().wait()
-
+    def to_row(self, chunk, slot):
         def step(i, c):
             pltpu.make_async_remote_copy(
-                src_ref=self.pair,
-                dst_ref=self.pair,
+                src_ref=chunk,
+                dst_ref=self.dst.at[slot],
                 send_sem=self.send_row,
                 recv_sem=self.recv_row,
                 device_id=row_peer(self.member, self.shard, i),
@@ -143,6 +136,16 @@
             return c
 
         lax.fori_loop(1, ROWS, step, 0)
+
+    def start(self):
+        self.swap().start()
+        self.to_row(self.src, self.shard)
+        self.local().start()
+
+    def relay(self):
+        self.local().wait()
+        self.swap().wait()
+        self.to_row(self.dst.at[self.partner], self.partner)
 
     def arrive(self):
         pltpu.make_async_copy(self.others, self.others, self.recv_row).wait()
@@ -253,20 +256,6 @@
         axis=0,
     ).astype(jnp.bfloat16)
     scatter_rows(normed(tokens[...], attn_gain[...]), h_src)
-    spread[...] = (head_key(iota((H * HD, 1), 0)) == cache_key()).astype(jnp.float32).astype(
-        jnp.bfloat16
-    )
-    column, real = context_column(iota((QUADS * packed, 1), 0))
-    gather[...] = (
-        (jnp.where(real, head_key(column), -1) == cache_key())
-        .astype(jnp.float32)
-        .astype(jnp.bfloat16)
-    )
-    lane = iota((2, 128), 1)
-    freqs = jnp.exp((lane & 31).astype(jnp.float32) * (-2.0 * math.log(10000.0) / HD))
-    angles = jnp.where(iota((2, 128), 0) == 0, lengths[0], lengths[1]).astype(jnp.float32) * freqs
-    cosine = jnp.cos(angles)
-    sine = jnp.sin(angles) * jnp.where((lane & 63) < 32, -1.0, 1.0)
     position = iota((1, CAP), 1)
     qkv_weights = Weights(qkv_src, wqkv_all, sems, 0, member, shard)
     out_weights = Weights(wout_src, wout_all, sems, 2, member, shard)
@@ -281,10 +270,21 @@
     pl.semaphore_wait(barrier, GROUP + ROWS - 1)
     qkv_weights.start()
     rows.start()
-    out_weights.start()
     qkv_weights.relay()
-    out_weights.relay()
-    ffn_weights.start()
+    spread[...] = (head_key(iota((H * HD, 1), 0)) == cache_key()).astype(jnp.float32).astype(
+        jnp.bfloat16
+    )
+    column, real = context_column(iota((QUADS * packed, 1), 0))
+    gather[...] = (
+        (jnp.where(real, head_key(column), -1) == cache_key())
+        .astype(jnp.float32)
+        .astype(jnp.bfloat16)
+    )
+    lane = iota((2, 128), 1)
+    freqs = jnp.exp((lane & 31).astype(jnp.float32) * (-2.0 * math.log(10000.0) / HD))
+    angles = jnp.where(iota((2, 128), 0) == 0, lengths[0], lengths[1]).astype(jnp.float32) * freqs
+    cosine = jnp.cos(angles)
+    sine = jnp.sin(angles) * jnp.where((lane & 63) < 32, -1.0, 1.0)
     rows.arrive()
     qkv_weights.arrive()
     product = jnp.dot(
@@ -294,7 +294,9 @@
     )
     qkv_part[...] = product.astype(jnp.bfloat16).reshape(GROUP, 2, 512)
     qkvs.start()
-    ffn_weights.relay()
+    out_weights.start()
+    out_weights.relay()
+    ffn_weights.start()
     qkvs.arrive()
     summed = jnp.sum(
         qkv_all[...].astype(jnp.float32).reshape(QUADS, 4, 2, 512), axis=0
@@ -321,6 +323,7 @@
     for quad in range(QUADS):
         ctx_src[quad] = context[:, quad * packed : (quad + 1) * packed]
     contexts.start()
+    ffn_weights.relay()
     contexts.arrive()
     out_weights.arrive()
     product = jnp.dot(

time: 71.5 us -> 69.6 us (0.973)
  Pallas kernels: 68.7 us -> 66.8 us
    pallas_call x1, Pallas kernels: 68.7 us -> 66.8 us  [body(): pl.pallas_call(layer_kernel, name='layer', out_shape=jax.ShapeDtypeStruct...]
where the time goes in v5:
time: 69.6 us; the launch traced here: 69.4 us
  Pallas kernels  66.8 us (96%)
  local copies, waits for them, and re-layouts  1.19 us (2%)
  other arithmetic  0.74 us (1%)
    pallas_call x1, Pallas kernels, body(): pl.pallas_call(layer_kernel, name='layer', out_shape=jax.ShapeDtypeStruct...  66.8 us

profile of v5, /device:TPU:1, one launch (start us, length us, event | category | flops | bytes accessed | tf_op | source)
XLA Modules:
  0.0 69.4 jit_solution(13732626432465613413)
XLA Ops:
  0.6 66.8 %layer.1 = f32[2,2688]{1,0:T(2,128)} custom-call(bf16[2,2048]{1,0:T(2,128)(2,1)} %tokens.1, s32[2]{0:T(128)} %lengths.1, f32[1,2048]{1,0:T(1,128)} %attn_gain.1, f32[1,2048]{1,0:T(1,128)} %mlp_gain.1, bf16[16,480]{1,0:T(8,128)(2,1)} %bitcast.16, bf16[10,512]{1,0:T(8,128)(2,1)} %bitcast.17, bf16[5,2048]{1,0:T(8,128)(2,1)} %bitcast.13, ...), custom_call_target="tpu_custom_call" | custom-call | tf_op jit(solution)/shard_map/layer/pallas_call | solution.py:395
  67.4 0.7 %convert_element_type.3 = bf16[2,2688]{1,0:T(2,128)(2,1)S(1)} convert(f32[2,2688]{1,0:T(2,128)} %layer.1) | non-fusion elementwise | flops 5376 | bytes 32256 | tf_op jit(solution)/shard_map/convert_element_type | solution.py:419
  68.2 0.6 slice_bitcast_fusion
  68.7 0.6 slice.8

commit v6 on v5

--- a/solution.py
+++ b/solution.py
@@ -152,6 +152,44 @@
 
     def sent(self):
         pltpu.make_async_copy(self.others, self.others, self.send_row).wait()
+
+
+class Phase:
+    def __init__(self, sems, k, member, shard):
+        self.plane, self.spot = lax.div(member, 8), lax.rem(member, 8)
+        self.base = shard * GROUP
+        self.send, self.recv, self.own = (s.at[k] for s in sems)
+
+    def remote(self, src, dst, peer):
+        pltpu.make_async_remote_copy(
+            src_ref=src,
+            dst_ref=dst,
+            send_sem=self.send,
+            recv_sem=self.recv,
+            device_id=device(self.base + peer),
+            device_id_type=MESH,
+        ).start()
+
+    def planes(self, src, dst):
+        def step(i, c):
+            plane = lax.rem(self.plane + i, 4)
+            self.remote(src(plane), dst, plane * 8 + self.spot)
+            return c
+
+        lax.fori_loop(1, 4, step, 0)
+
+    def spots(self, copy):
+        def step(i, c):
+            spot = lax.rem(self.spot + i, 8)
+            copy(spot, self.plane * 8 + spot)
+            return c
+
+        lax.fori_loop(1, 8, step, 0)
+
+
+def await_slots(buffer, count, sem):
+    slots = buffer.at[pl.ds(0, count)]
+    pltpu.make_async_copy(slots, slots, sem).wait()
 
 
 def iota(shape, axis):
@@ -239,7 +277,7 @@
     out_ref,
     kv, h_src, h_all, qkv_src, wqkv_all, wout_src, wout_all, ffn_src, ffn_all,
     qkv_part, qkv_all, ctx_src, ctx_all, out_part, out_all,
-    second, second_all, down, down_all, spread, gather, joint, kv_sem, *sems
+    second, second_all, down, down_all, spread, gather, joint, folded, folded_all, kv_sem, *sems
 ):
     member, shard = place()
     packed = SHARDS * TILE
@@ -264,8 +302,10 @@
     qkvs = Transfer(lambda peer: qkv_part.at[peer], qkv_all, sems, 7, member, shard)
     contexts = Transfer(lambda peer: ctx_src.at[lax.div(peer, 4)], ctx_all, sems, 8, member, shard)
     outs = Transfer(lambda peer: out_part.at[peer], out_all, sems, 9, member, shard)
-    seconds = Transfer(lambda peer: second, second_all, sems, 10, member, shard)
-    downs = Transfer(lambda peer: down.at[peer], down_all, sems, 11, member, shard)
+    across = Phase(sems, 10, member, shard)
+    within = Phase(sems, 11, member, shard)
+    fold = Phase(sems, 12, member, shard)
+    last = Phase(sems, 13, member, shard)
 
     pl.semaphore_wait(barrier, GROUP + ROWS - 1)
     qkv_weights.start()
@@ -340,8 +380,20 @@
     projected = jnp.concatenate([projected[x] for x in range(4)], axis=-1)
     after_attn = (tokens[...].astype(jnp.float32) + projected).astype(jnp.bfloat16)
     second[...] = normed(after_attn, mlp_gain[...]).astype(jnp.bfloat16)
-    seconds.start()
-    seconds.arrive()
+    across.planes(lambda plane: second, second_all.at[member])
+    within.spots(lambda spot, peer: within.remote(second, second_all.at[member], peer))
+    mine = pltpu.make_async_copy(second, second_all.at[member], across.own)
+    mine.start()
+    await_slots(second_all, 3, across.recv)
+
+    def forward(spot, peer):
+        for i in range(1, 4):
+            slot = second_all.at[lax.rem(within.plane + i, 4) * 8 + within.spot]
+            within.remote(slot, slot, peer)
+
+    within.spots(forward)
+    mine.wait()
+    await_slots(second_all, 28, within.recv)
     ffn_weights.arrive()
     ffn = ffn_all[...].reshape(packed, 2048)
     gate_up = lax.dot_general(
@@ -356,19 +408,40 @@
     hidden = jnp.where((lane >= 10) & (lane < 15), hidden, 0.0).astype(jnp.bfloat16)
     product = jnp.dot(hidden, ffn, preferred_element_type=jnp.float32)
     down[...] = product.astype(jnp.bfloat16).reshape(GROUP, 2, 2048)
-    downs.start()
-    downs.arrive()
-    total = jnp.sum(down_all[...].astype(jnp.float32), axis=0)
+
+    def spread_down(spot, peer):
+        for plane in range(4):
+            fold.remote(down.at[plane * 8 + spot], down_all.at[plane * 8 + fold.spot], peer)
+
+    fold.spots(spread_down)
+    for plane in range(4):
+        slot = plane * 8 + fold.spot
+        pltpu.make_async_copy(down.at[slot], down_all.at[slot], fold.own).start()
+    await_slots(down_all, 4, fold.own)
+    await_slots(down_all, 28, fold.recv)
+    folded[...] = jnp.sum(
+        down_all[...].astype(jnp.float32).reshape(4, 8, 2, 2048), axis=1
+    )
+    last.planes(lambda plane: folded.at[plane], folded_all.at[last.plane])
+    mine = pltpu.make_async_copy(folded.at[last.plane], folded_all.at[last.plane], last.own)
+    mine.start()
+    mine.wait()
+    await_slots(folded_all, 3, last.recv)
+    total = jnp.sum(folded_all[...], axis=0)
     stream = (after_attn.astype(jnp.float32) + total).astype(jnp.bfloat16)
     out_ref[:, :2048] = stream.astype(jnp.float32)
-    for transfer in (qkv_weights, out_weights, ffn_weights, rows, qkvs, contexts, outs, seconds, downs):
+    for transfer in (qkv_weights, out_weights, ffn_weights, rows, qkvs, contexts, outs):
         transfer.sent()
+    await_slots(second_all, 3, across.send)
+    await_slots(second_all, 28, within.send)
+    await_slots(down_all, 28, fold.send)
+    await_slots(folded_all, 3, last.send)
 
 
 def body(tokens, cache_lengths, kv_cache, attn_gain, mlp_gain, w_qkv, w_out, w_gate, w_up, w_down):
     packed = SHARDS * TILE
     vmem = pl.BlockSpec(memory_space=pltpu.VMEM)
-    transfers = 12
+    transfers = 14
     shapes = [
         (2, CAP, 640),
         (QUADS, 2, packed),
@@ -401,7 +474,9 @@
         + [pl.BlockSpec(memory_space=pl.ANY)],
         out_specs=vmem,
         scratch_shapes=[pltpu.VMEM(shape, jnp.bfloat16) for shape in shapes]
-        + [pltpu.VMEM((2, 1920), jnp.float32), pltpu.SemaphoreType.DMA((1,))]
+        + [pltpu.VMEM((2, 1920), jnp.float32)]
+        + [pltpu.VMEM((4, 2, 2048), jnp.float32)] * 2
+        + [pltpu.SemaphoreType.DMA((1,))]
         + [pltpu.SemaphoreType.DMA((transfers,))] * 3,
         compiler_params=pltpu.CompilerParams(collective_id=0, has_side_effects=True),
     )(

time: 69.6 us -> 71 us (1.020)
  Pallas kernels: 66.8 us -> 68.1 us
    pallas_call x1, Pallas kernels: 66.8 us -> 68.1 us  [body(): pl.pallas_call(layer_kernel, name='layer', out_shape=jax.ShapeDtypeStruct...]
where the time goes in v6:
time: 71 us; the launch traced here: 70.7 us
  Pallas kernels  68.1 us (96%)
  local copies, waits for them, and re-layouts  1.19 us (2%)
  other arithmetic  0.74 us (1%)
    pallas_call x1, Pallas kernels, body(): pl.pallas_call(layer_kernel, name='layer', out_shape=jax.ShapeDtypeStruct...  68.1 us

profile of v6, /device:TPU:1, one launch (start us, length us, event | category | flops | bytes accessed | tf_op | source)
XLA Modules:
  0.0 70.7 jit_solution(6298194706945618761)
XLA Ops:
  0.6 68.1 %layer.1 = f32[2,2688]{1,0:T(2,128)} custom-call(bf16[2,2048]{1,0:T(2,128)(2,1)} %tokens.1, s32[2]{0:T(128)} %lengths.1, f32[1,2048]{1,0:T(1,128)} %attn_gain.1, f32[1,2048]{1,0:T(1,128)} %mlp_gain.1, bf16[16,480]{1,0:T(8,128)(2,1)} %bitcast.16, bf16[10,512]{1,0:T(8,128)(2,1)} %bitcast.17, bf16[5,2048]{1,0:T(8,128)(2,1)} %bitcast.13, ...), custom_call_target="tpu_custom_call" | custom-call | tf_op jit(solution)/shard_map/layer/pallas_call | solution.py:468
  68.8 0.7 %convert_element_type.3 = bf16[2,2688]{1,0:T(2,128)(2,1)S(1)} convert(f32[2,2688]{1,0:T(2,128)} %layer.1) | non-fusion elementwise | flops 5376 | bytes 32256 | tf_op jit(solution)/shard_map/convert_element_type | solution.py:494
  69.5 0.6 slice_bitcast_fusion
  70.1 0.6 slice.8
